TPU v7x, 256 devices: a whole 4x4x8 slice. The times are simulated.
256 devices in a mesh: expert: 32 (over y, z_hi, x), dp: 8 (over z_lo, core).
Axes of the slice: x: 4, y: 4, z: 8 (z_hi: 2, z_lo: 4; z = z_hi * 4 + z_lo), core: 2. Of those that a mesh axis runs over, the one named last changes fastest.
Arguments:
- tokens: bfloat16 [8192, 3584], P('expert'), may hold values from -6 to 6
- expert_ids: int32 [8192, 8], P('expert'), may hold values from 0 to 255, all different within a row; in each aligned block of 256 rows (0 to 255, 256 to 511, ...) at most 16 rows name the same one
- gate_values: float32 [8192, 8], P('expert'), may hold values from 0.1 to 1
- tiles: int32 [32], P('expert'), may hold values from 1 to 2
- w_gate: bfloat16 [32, 3584, 2048], P('expert', None, 'dp'), may hold values from -0.09375 to 0.09375
- w_up: bfloat16 [32, 3584, 2048], P('expert', None, 'dp'), may hold values from -0.09375 to 0.09375
- w_down: bfloat16 [32, 2048, 3584], P('expert', 'dp'), may hold values from -0.125 to 0.125
- grad_out: bfloat16 [8192, 3584], P('expert', 'dp'), may hold values from -6 to 6
Outputs:
- mixed: bfloat16 [8192, 3584], P('expert', 'dp')
- grad_tokens: bfloat16 [8192, 3584], P('expert', 'dp')
- grad_gates: float32 [8192, 8], P('expert')
- grad_w_gate: bfloat16 [32, 3584, 2048], P('expert', None, 'dp')
- grad_w_up: bfloat16 [32, 3584, 2048], P('expert', None, 'dp')
- grad_w_down: bfloat16 [32, 2048, 3584], P('expert', 'dp')
Inputs may be any that keep to these rules, and one draw needn't show every extreme that they name: `expert_ids`: each row names 8 different experts. Within the rows of one device (aligned blocks of 256 rows) no expert is named by more than 16 rows.
All inputs are finite; a program needn't handle non-finite values.
Results may differ from a plain program's by a relative error of at most 0.015.
Values may be sent and summed in bfloat16 or wider, within the bound.
A program may use at most 128 MiB of HBM per device.

v0:
```python
import jax
import jax.numpy as jnp
from jax import lax
from jax.sharding import PartitionSpec as P

TILE = 128
SLOTS = 16


def route_tables(ids, gates, count, experts, slots, tile):
    tok, top = ids.shape
    queue = experts * slots
    live = jnp.arange(tok, dtype=jnp.int32) < count * tile
    valid = (ids < experts) & live[:, None]
    flat_ids = ids.reshape(-1)
    flat_valid = valid.reshape(-1)
    onehot = (
        (flat_ids[:, None] == jnp.arange(experts, dtype=jnp.int32)[None, :]) & flat_valid[:, None]
    ).astype(jnp.int32)
    ranks = jnp.sum((jnp.cumsum(onehot, axis=0) - 1) * onehot, axis=1)
    target = jnp.where(flat_valid, flat_ids * slots + ranks, -1)
    match = (target[None, :] == jnp.arange(queue, dtype=jnp.int32)[:, None]).astype(jnp.float32)
    picker = jnp.sum(match.reshape(queue, tok, top), axis=2)
    slot_gate = jnp.dot(match, gates.reshape(-1), precision=lax.Precision.HIGHEST)
    return (match, picker, slot_gate)


def spread_rows(picker_tb, values):
    upper = values.astype(jnp.bfloat16)
    lower = (values - upper.astype(jnp.float32)).astype(jnp.bfloat16)
    return jnp.dot(picker_tb, upper, preferred_element_type=jnp.float32) + jnp.dot(
        picker_tb, lower, preferred_element_type=jnp.float32
    )


def on_device(tokens, expert_ids, gate_values, tiles, w_gate, w_up, w_down, grad_out):
    experts = lax.axis_size("expert")
    tok_rows, width = tokens.shape
    top = expert_ids.shape[1]
    queue = experts * SLOTS
    match, picker, slot_gate = route_tables(expert_ids, gate_values, tiles[0], experts, SLOTS, TILE)
    pick_b = picker.astype(jnp.bfloat16)
    picker_tb = picker.T.astype(jnp.bfloat16)
    gathered = (
        jnp.dot(pick_b, tokens, preferred_element_type=jnp.float32)
        .astype(jnp.bfloat16)
        .reshape(experts, SLOTS, width)
    )
    arrived = lax.all_to_all(gathered, "expert", split_axis=0, concat_axis=0, tiled=True)
    rows = arrived.reshape(queue, width)
    w_g = w_gate[0]
    w_u = w_up[0]
    w_d = w_down[0]
    gate_pre = jnp.dot(rows, w_g, preferred_element_type=jnp.float32)
    up_pre = jnp.dot(rows, w_u, preferred_element_type=jnp.float32)
    sig = jax.nn.sigmoid(gate_pre)
    hidden = (gate_pre * sig * up_pre).astype(jnp.bfloat16)
    partial_value = jnp.dot(hidden, w_d, preferred_element_type=jnp.float32)
    returned = (
        lax.all_to_all(
            partial_value.reshape(experts, SLOTS, width).astype(jnp.bfloat16),
            "expert",
            split_axis=0,
            concat_axis=0,
            tiled=True,
        )
        .astype(jnp.float32)
        .reshape(queue, width)
    )
    token_part = spread_rows(picker_tb, returned * slot_gate[:, None])
    mixed = lax.psum_scatter(token_part.astype(jnp.bfloat16), "dp", scatter_dimension=1, tiled=True)
    dy_full = lax.all_gather(grad_out, "dp", axis=1, tiled=True)
    dy_rows = jnp.dot(pick_b, dy_full, preferred_element_type=jnp.float32)
    score = lax.psum(jnp.sum(dy_rows * returned, axis=1), "dp")
    dyrow = (dy_rows * slot_gate[:, None]).astype(jnp.bfloat16).reshape(experts, SLOTS, width)
    dy_arrived = lax.all_to_all(dyrow, "expert", split_axis=0, concat_axis=0, tiled=True)
    dy_slots = dy_arrived.reshape(queue, width)
    d_hidden = jnp.dot(dy_slots, w_d.T, preferred_element_type=jnp.float32)
    d_gate = (d_hidden * up_pre * sig * (1.0 + gate_pre * (1.0 - sig))).astype(jnp.bfloat16)
    d_up = (d_hidden * gate_pre * sig).astype(jnp.bfloat16)
    grad_down = jnp.dot(hidden.T, dy_slots, preferred_element_type=jnp.float32).astype(jnp.bfloat16)
    grad_gate = jnp.dot(rows.T, d_gate, preferred_element_type=jnp.float32).astype(jnp.bfloat16)
    grad_up = jnp.dot(rows.T, d_up, preferred_element_type=jnp.float32).astype(jnp.bfloat16)
    input_rows = jnp.dot(d_gate, w_g.T, preferred_element_type=jnp.float32) + jnp.dot(
        d_up, w_u.T, preferred_element_type=jnp.float32
    )
    input_back = (
        lax.all_to_all(
            input_rows.reshape(experts, SLOTS, width).astype(jnp.bfloat16),
            "expert",
            split_axis=0,
            concat_axis=0,
            tiled=True,
        )
        .astype(jnp.float32)
        .reshape(queue, width)
    )
    token_grad = spread_rows(picker_tb, input_back)
    grad_tokens = lax.psum_scatter(
        token_grad.astype(jnp.bfloat16), "dp", scatter_dimension=1, tiled=True
    )
    grad_gates = jnp.dot(score, match, precision=lax.Precision.HIGHEST).reshape(tok_rows, top)
    return (mixed, grad_tokens, grad_gates, grad_gate[None], grad_up[None], grad_down[None])


def solution(mesh):
    placed = (
        P("expert", None),
        P("expert", None),
        P("expert", None),
        P("expert"),
        P("expert", None, "dp"),
        P("expert", None, "dp"),
        P("expert", "dp", None),
        P("expert", "dp"),
    )
    return jax.shard_map(
        on_device,
        mesh=mesh,
        in_specs=placed,
        out_specs=(
            P("expert", "dp"),
            P("expert", "dp"),
            P("expert", None),
            P("expert", None, "dp"),
            P("expert", None, "dp"),
            P("expert", "dp", None),
        ),
        check_vma=False,
    )
```

profile of v0, /device:TPU:97, one launch (start us, length us, event | category | flops | bytes accessed | tf_op | source)
XLA Modules:
  0.0 477.3 jit_solution(10951024635120724475)
XLA Ops:
  7.2 0.0 copy-start
  8.0 0.7 compare_and_fusion
  8.7 0.2 copy.37
  8.9 0.1 and.28
  9.0 0.1 and.31
  9.1 0.8 copy.36
  9.9 0.1 eq.45
  10.0 0.1 eq.49
  10.2 9.1 %reduce-window.6 = s32[32,16,128]{2,1,0:T(8,128)S(1)} reduce-window(s32[32,16,128]{2,1,0:T(8,128)S(1)} %fusion.29, s32[]{:T(128)} %constant.6.clone.1), window={size=1x1x128 pad=0_0x0_0x127_0}, to_apply=%region_0.0 | reduce-window | flops 8323072 | bytes 524292 | tf_op jit(solution)/shard_map/reduce-window
  19.3 0.1 slice.8
  19.4 0.2 copy.45
  19.6 0.2 reduce-window.9
  19.8 0.1 add_add_fusion
  20.0 0.1 fusion.26
  20.1 0.1 reduce_sum.30
  20.2 0.1 copy.42
  20.3 0.7 add_select_fusion.1
  21.0 1.9 convert_reduce_fusion
  22.9 2.6 convolution_convert_fusion.1
  25.5 0.0 copy-start.6
  25.5 74.1 %all_to_all.20 = bf16[32,16,3584]{2,1,0:T(8,128)(2,1)S(1)} all-to-all(bf16[32,16,3584]{2,1,0:T(8,128)(2,1)S(1)} %bitcast.84), channel_id=1, replica_groups=mesh['expert'=32,'dp'=8] {'expert'}, dimensions={0} | all-to-all | bytes 7340032 | tf_op jit(solution)/shard_map/all_to_all | solution.py:49
  99.6 0.0 copy-done.6
  99.6 1.1 fusion.23
  100.8 1.7 copy-done.8
  102.5 1.9 multiply_convert_fusion.3
  104.4 0.0 copy-done.4
  104.4 0.0 copy-done
  104.4 3.0 convolution_convert_fusion
  107.4 5.0 %all-to-all-start.1 = ((bf16[32,16,3584]{2,1,0:T(8,128)(2,1)}), bf16[32,16,3584]{2,1,0:T(8,128)(2,1)}, u32[]{:S(2)}, u32[]{:S(2)}) async-start(bf16[32,16,3584]{2,1,0:T(8,128)(2,1)} %convolution_convert_fusion), calls=%async_computation.1 | async-start | bytes 7340032 | tf_op jit(solution)/shard_map/all_to_all | solution.py:60
  112.4 0.0 all-gather.2.cloned.1.call-start
  112.4 0.7 all-gather.2.cloned.1.call-update
  113.1 0.0 copy-done.10
  113.1 0.1 copy.43
  113.3 0.1 reshape.117
  113.4 1.9 fusion.10
  115.3 87.7 %all-gather.2.cloned.1.call-done = bf16[256,3584]{0,1:T(8,128)(2,1)} async-done(((bf16[256,448]{0,1:T(8,128)(2,1)}), bf16[256,3584]{0,1:T(8,128)(2,1)}) %all-gather.2.cloned.1.call-update) | async-done | bytes 1835024 | tf_op jit(solution)/shard_map/all_gather | solution.py:72
  203.0 0.0 all-to-all-done.1
  203.0 5.5 %fusion.3 = (f32[512]{0:T(512)S(1)}, bf16[512,3584]{1,0:T(8,128)(2,1)S(1)}, bf16[512,3584]{1,0:T(8,128)(2,1)}) fusion(bf16[32,16,3584]{2,1,0:T(8,128)(2,1)} %all-to-all-done.1, f32[512]{0:T(512)S(1)} %bitcast.96, bf16[512,256]{1,0:T(8,128)(2,1)S(1)} %convert_reduce_fusion, bf16[256,3584]{0,1:T(8,128)(2,1)} %all-gather.2.cloned.1.call-done), kind=kOutput, calls=%fused_computation.5 | convolution fusion | flops 952368640 | bytes 13111296 | tf_op jit(solution)/shard_map/dot_general | solution.py:73
  208.5 114.1 %all_to_all.21 = bf16[32,16,3584]{2,1,0:T(8,128)(2,1)S(1)} all-to-all(bf16[32,16,3584]{2,1,0:T(8,128)(2,1)S(1)} %bitcast.89), channel_id=1, replica_groups=mesh['expert'=32,'dp'=8] {'expert'}, dimensions={0} | all-to-all | bytes 7340032 | tf_op jit(solution)/shard_map/all_to_all | solution.py:76
  322.6 1.2 multiply_convert_fusion.1
  323.9 0.7 copy-done.2
  324.5 0.9 copy-done.7
  325.5 1.2 fusion.21
  326.6 0.3 copy-done.9
  327.0 3.1 add_convert_fusion
  330.1 7.9 %all-to-all-start.3 = ((bf16[32,16,3584]{2,1,0:T(8,128)(2,1)}), bf16[32,16,3584]{2,1,0:T(8,128)(2,1)}, u32[]{:S(2)}, u32[]{:S(2)}) async-start(bf16[32,16,3584]{2,1,0:T(8,128)(2,1)} %bitcast.83), calls=%async_computation.4 | async-start | bytes 7340032 | tf_op jit(solution)/shard_map/all_to_all | solution.py:88
  338.0 0.0 reduce-scatter.3.cloned.1.call-start
  338.0 0.0 copy-start.3
  338.0 3.8 fusion.30
  341.8 5.6 %fusion.4 = bf16[256,3584]{0,1:T(8,128)(2,1)} fusion(f32[256,3584]{0,1:T(8,128)S(1)} %fusion.30, bf16[512,256]{1,0:T(8,128)(2,1)S(1)} %convert_reduce_fusion, bf16[512,3584]{1,0:T(8,128)(2,1)} %bitcast.17, bf16[512,3584]{1,0:T(8,128)(2,1)S(1)} %copy-done.3, f32[512]{0:T(512)S(1)} %bitcast.97), kind=kOutput, calls=%fused_computation.13 | convolution fusion | flops 950534144 | bytes 13109248 | tf_op jit(solution)/shard_map/dot_general | solution.py:31
  347.4 0.0 reduce-scatter.3.cloned.1.call-update
  347.4 0.0 reduce-scatter.5.cloned.1.call-start
  347.5 78.1 %all-to-all-done.3 = bf16[32,16,3584]{2,1,0:T(8,128)(2,1)} async-done(((bf16[32,16,3584]{2,1,0:T(8,128)(2,1)}), bf16[32,16,3584]{2,1,0:T(8,128)(2,1)}, u32[]{:S(2)}, u32[]{:S(2)}) %all-to-all-start.3) | async-done | bytes 3670048 | tf_op jit(solution)/shard_map/all_to_all | solution.py:88
  425.5 3.6 fusion.31
  429.2 5.0 %fusion.5 = bf16[256,3584]{0,1:T(8,128)(2,1)} fusion(f32[256,3584]{0,1:T(8,128)S(1)} %fusion.31, bf16[512,256]{1,0:T(8,128)(2,1)S(1)} %convert_reduce_fusion, bf16[512,3584]{1,0:T(8,128)(2,1)} %bitcast.16), kind=kOutput, calls=%fused_computation.14 | convolution fusion | flops 946864128 | bytes 9437184 | tf_op jit(solution)/shard_map/dot_general | solution.py:31
  434.1 0.0 reduce-scatter.5.cloned.1.call-update
  434.2 13.3 %psum.7 = f32[512]{0:T(512)S(1)} all-reduce(f32[512]{0:T(512)S(1)} %get-tuple-element.24), channel_id=1, replica_groups=mesh['expert'=32,'dp'=8] {'dp'}, use_global_device_ids=true, to_apply=%region_7.8 | all-reduce | flops 512 | bytes 4096 | tf_op jit(solution)/shard_map/psum | solution.py:74
  447.5 1.4 fusion.9
  448.9 0.1 reshape.113
  449.0 0.7 copy.44
  449.7 4.6 fusion.8
  454.2 2.4 fusion.7
  456.6 2.4 fusion.6
  459.0 11.8 %reduce-scatter.5.cloned.1.call-done = bf16[256,448]{0,1:T(8,128)(2,1)} async-done(((bf16[256,3584]{0,1:T(8,128)(2,1)}), bf16[256,448]{0,1:T(8,128)(2,1)}) %reduce-scatter.5.cloned.1.call-update) | async-done | bytes 229392 | tf_op jit(solution)/shard_map/reduce_scatter | solution.py:99
  (17 shorter events, 0.1 us)
Async XLA Ops:
  7.2 97.2 %copy-start = (bf16[1,256,3584]{2,1,0:T(8,128)(2,1)S(1)}, bf16[1,256,3584]{2,1,0:T(8,128)(2,1)}, u32[]{:S(2)}) copy-start(bf16[1,256,3584]{2,1,0:T(8,128)(2,1)} %param.14) | copy-start | bytes 5505028
  25.5 74.1 %copy-start.6 = (bf16[1,3584,256]{2,1,0:T(8,128)(2,1)S(1)}, bf16[1,3584,256]{2,1,0:T(8,128)(2,1)}, u32[]{:S(2)}) copy-start(bf16[1,3584,256]{2,1,0:T(8,128)(2,1)} %param.12) | copy-start | bytes 5505028
  99.6 4.7 copy-start.4
  99.6 2.8 copy-start.8
  107.4 5.7 %copy-start.10 = (f32[256,8]{0,1:T(8,128)S(1)}, f32[256,8]{0,1:T(8,128)}, u32[]{:S(2)}) copy-start(f32[256,8]{0,1:T(8,128)} %param.10) | copy-start | bytes 24580
  107.4 95.6 %all-to-all-start.1 = ((bf16[32,16,3584]{2,1,0:T(8,128)(2,1)}), bf16[32,16,3584]{2,1,0:T(8,128)(2,1)}, u32[]{:S(2)}, u32[]{:S(2)}) async-start(bf16[32,16,3584]{2,1,0:T(8,128)(2,1)} %convolution_convert_fusion), calls=%async_computation.1 | async-start | bytes 7340032 | tf_op jit(solution)/shard_map/all_to_all | solution.py:60
  112.4 90.6 %all-gather.2.cloned.1.call-start = ((), (), s32[]{:S(2)}) async-start(), calls=%async_computation.7 | async-start | bytes 2064384 | tf_op jit(solution)/shard_map/all_gather | solution.py:72
  208.5 114.1 %copy-start.11 = (f32[512,256]{1,0:T(8,128)S(1)}, f32[512,256]{1,0:T(8,128)}, u32[]{:S(2)}) copy-start(f32[512,256]{1,0:T(8,128)} %get-tuple-element.30) | copy-start | bytes 1572868
  322.6 1.9 copy-start.2
  322.6 2.8 copy-start.7
  325.5 1.5 copy-start.9
  330.1 95.4 %all-to-all-start.3 = ((bf16[32,16,3584]{2,1,0:T(8,128)(2,1)}), bf16[32,16,3584]{2,1,0:T(8,128)(2,1)}, u32[]{:S(2)}, u32[]{:S(2)}) async-start(bf16[32,16,3584]{2,1,0:T(8,128)(2,1)} %bitcast.83), calls=%async_computation.4 | async-start | bytes 7340032 | tf_op jit(solution)/shard_map/all_to_all | solution.py:88
  338.0 121.1 %reduce-scatter.3.cloned.1.call-start = ((), (), s32[]{:S(2)}) async-start(), calls=%async_computation.6 | async-start | bytes 2064384 | tf_op jit(solution)/shard_map/reduce_scatter | solution.py:71
  338.0 3.8 copy-start.3
  347.4 123.4 %reduce-scatter.5.cloned.1.call-start = ((), (), s32[]{:S(2)}) async-start(), calls=%async_computation.8 | async-start | bytes 2064384 | tf_op jit(solution)/shard_map/reduce_scatter | solution.py:99
  449.7 4.6 copy-start.5
  454.2 16.6 %copy-start.1 = (bf16[1,256,3584]{2,1,0:T(8,128)(2,1)S(1)}, bf16[1,256,3584]{2,1,0:T(8,128)(2,1)}, u32[]{:S(2)}) copy-start(bf16[1,256,3584]{2,1,0:T(8,128)(2,1)} %param.14) | copy-start | bytes 5505028
Sparse Core Ops, SparseCore 0:
  115.0 87.9 all-gather.1
  347.5 67.3 reduce-scatter.2
  434.3 36.4 reduce-scatter.4
where the time goes:
time: 482 us; the launch traced here: 477 us
  blocking collectives  202 us (42%)
  waiting for transfers between devices  178 us (37%)
  matrix products  50.3 us (10%)
  between operations  14.7 us (3%)
  starting transfers between devices  13 us (3%)
  other arithmetic  12.9 us (3%)
  local copies, waits for them, and re-layouts  6.68 us (1%)
    all_to_all x1, blocking collectives, on_device(): lax.all_to_all(dyrow, 'expert', split_axis=0, concat_axis=0, tiled=True)  114 us
    all_gather x1, waiting for transfers between devices, on_device(): dy_full = lax.all_gather(grad_out, 'dp', axis=1, tiled=True)  87.7 us
    all_to_all x1, waiting for transfers between devices, on_device(): lax.all_to_all(input_rows.reshape(experts, SLOTS, width).astype(jnp.bfloa...  78.1 us
    all_to_all x1, blocking collectives, on_device(): lax.all_to_all(gathered, 'expert', split_axis=0, concat_axis=0, tiled=True)  74.1 us
    psum x1, blocking collectives, on_device(): score = lax.psum(jnp.sum(dy_rows * returned, axis=1), 'dp')  13.3 us
    reduce_scatter x1, waiting for transfers between devices, on_device(): lax.psum_scatter(token_grad.astype(jnp.bfloat16), 'dp', scatter_dimension...  11.8 us
    dot_general x2, matrix products, spread_rows(): jnp.dot(picker_tb, lower, preferred_element_type=jnp.float32)  10.5 us
  transfers between devices with their start and end apart: 5, of which 3 were waited for; matrix products, arithmetic and copies ran while one was open for 7% of the time, Pallas kernels for 0%

commit v1 on v0

v1 whole, which is shorter than its diff:
```python
import functools

import jax
import jax.numpy as jnp
from jax import lax
from jax.experimental import pallas as pl
from jax.experimental.pallas import tpu as pltpu
from jax.sharding import PartitionSpec as P

TILE = 128
SL = 16
MESH = pl.DeviceIdType.MESH
VMEM_LIMIT = 60 * 1024 * 1024
BF = jnp.bfloat16
F32 = jnp.float32
ROWBLOCKS = 4


def place(nx):
    e = lax.axis_index("expert")
    d = lax.axis_index("dp")
    x = lax.rem(e, nx)
    zh = lax.rem(lax.div(e, nx), 2)
    y = lax.div(e, 2 * nx)
    return y * nx + x, zh, lax.div(d, 2), lax.rem(d, 2)


def device(nx, q, z, core):
    e = (lax.div(q, nx) * 2 + lax.div(z, 4)) * nx + lax.rem(q, nx)
    return {"expert": e, "dp": lax.rem(z, 4) * 2 + core}


def signal(sem, who):
    pl.semaphore_signal(sem, inc=1, device_id=who, device_id_type=MESH)


def remote(src, dst, send, recv, who):
    return pltpu.make_async_remote_copy(
        src_ref=src, dst_ref=dst, send_sem=send, recv_sem=recv, device_id=who, device_id_type=MESH
    )


def dispatch_kernel(
    nx, nq, tok_ref, gout_ref, tabs_ref, x_ref, dy_ref, tab_ref,
    tok, tabr, dyt, rows, pick, sg,
    tok_l, tab_l, gout_l, row_l, tab_s, tab_r, gout_s, gout_r, x_s, x_r, up_s, down_s, ring_r,
    plane_s, plane_r, sib_s, sib_r,
):
    me, zh, zl, c = place(nx)
    z = zh * 4 + zl
    own = zh == c
    r = lax.rem(z - 4 * c + 8, 8)
    ntok = tok_ref.shape[0]
    ch = gout_ref.shape[1]
    pair = 2 * ch
    ns = nq * SL
    up = device(nx, me, lax.rem(z + 1, 8), c)
    down = device(nx, me, lax.rem(z + 7, 8), c)
    across = device(nx, me, lax.rem(z + 4, 8), c)
    sibling = device(nx, me, z, 1 - c)
    outs = (x_ref, dy_ref)

    barrier = pltpu.get_barrier_semaphore()
    for who in (up, down, across, sibling):
        signal(barrier, who)

    @pl.loop(1, nq)
    def _(i):
        signal(barrier, device(nx, lax.rem(me + i, nq), z, c))

    pl.semaphore_wait(barrier, 4 + nq - 1)

    def tok_in(g):
        return pltpu.make_async_copy(tok_ref.at[:, pl.ds(g * pair, pair)], tok.at[g], tok_l.at[g])

    tab_in = pltpu.make_async_copy(tabs_ref.at[zh], tabr, tab_l)
    tab_out = remote(tabs_ref.at[1 - zh], tabr, tab_s, tab_r, across)
    mine = 2 * zl + c
    gout_in = pltpu.make_async_copy(gout_ref, dyt.at[mine], gout_l)
    gout_out = remote(gout_ref, dyt.at[mine], gout_s, gout_r, sibling)

    def piece(h, i, who):
        step = ntok // ROWBLOCKS
        part = tok.at[2 * h + i // ROWBLOCKS, pl.ds((i % ROWBLOCKS) * step, step)]
        return remote(part, part, x_s.at[h, i], x_r.at[h, i], who)

    def ring(j, who, sems):
        part = dyt.at[pl.ds(2 * j, 2)]
        return remote(part, part, sems.at[j], ring_r.at[j], who)

    pieces = 2 * ROWBLOCKS

    @pl.when(own)
    def _():
        tab_out.start()
        tab_in.start()
        gout_in.start()
        for g in (0, 2, 1, 3):
            tok_in(g).start()
        gout_in.wait()
        gout_out.wait_recv()
        ring(zl, up, up_s).start()
        ring(zl, down, down_s).start()
        for g in (0, 2, 1, 3):
            tok_in(g).wait()
            for i in range(ROWBLOCKS):
                n = (g % 2) * ROWBLOCKS + i
                if g < 2:

                    @pl.when(r == 3)
                    def _():
                        piece(0, n, up).start()
                else:

                    @pl.when(r == 0)
                    def _():
                        piece(1, n, down).start()

        tab_in.wait()

    @pl.when(jnp.logical_not(own))
    def _():
        gout_out.start()
        tab_out.wait_recv()

    rt = tabr[0:nq, :]
    gt = tabr[nq : 2 * nq, :]
    slot = lax.broadcasted_iota(jnp.int32, (nq, SL, ntok), 1).astype(F32)
    hit = jnp.where(jnp.broadcast_to(rt[:, None, :], (nq, SL, ntok)) == slot, 1.0, 0.0)
    pick[...] = hit.reshape(ns, ntok).astype(BF)
    weighted = hit * jnp.broadcast_to(gt[:, None, :], (nq, SL, ntok))
    sg[...] = jnp.broadcast_to(jnp.sum(weighted.reshape(ns, ntok), axis=1, keepdims=True), sg.shape)
    tab_ref[...] = tabr[...]

    def send_rows(t, g):
        @pl.loop(1, nq)
        def _(i):
            q = lax.rem(me + i, nq)
            remote(
                rows.at[t, g, pl.ds(pl.multiple_of(q * SL, SL), SL)],
                outs[t].at[g, pl.ds(pl.multiple_of(c * ns + me * SL, SL), SL)],
                plane_s.at[t, g], plane_r.at[t, g], device(nx, q, z, c),
            ).start()

        row_local(t, g).start()

    def row_local(t, g):
        return pltpu.make_async_copy(
            rows.at[t, g, pl.ds(pl.multiple_of(me * SL, SL), SL)],
            outs[t].at[g, pl.ds(pl.multiple_of(c * ns + me * SL, SL), SL)],
            row_l.at[t, g],
        )

    def x_group(g):
        rows[0, g] = jnp.dot(pick[...], tok[g], preferred_element_type=F32).astype(BF)
        send_rows(0, g)

    def dy_group(g):
        a = jnp.dot(pick[...], dyt[2 * g], preferred_element_type=F32)
        b = jnp.dot(pick[...], dyt[2 * g + 1], preferred_element_type=F32)
        both = jnp.concatenate([a, b], axis=1)
        rows[1, g] = (both * sg[:, 0:1]).astype(BF)
        send_rows(1, g)

    @pl.when(own)
    def _():
        @pl.loop(0, 4)
        def _(g):
            x_group(g)

        dy_group(zl)

    @pl.when(jnp.logical_not(own))
    def _():
        for i in range(pieces):
            piece(0, i, up).wait_recv()

            @pl.when(r < 7)
            def _():
                piece(0, i, up).start()

            piece(1, i, down).wait_recv()

            @pl.when(r > 4)
            def _():
                piece(1, i, down).start()

            if i % ROWBLOCKS == ROWBLOCKS - 1:
                x_group(i // ROWBLOCKS)
                x_group(2 + i // ROWBLOCKS)

    @pl.loop(1, 5)
    def _(k):
        ju = lax.rem(r - k + 8, 8)
        jd = lax.rem(r + k, 8)
        from_below = ju < 4
        from_above = jnp.logical_and(jd < 4, k < 4)

        @pl.when(from_below)
        def _():
            ring(ju, up, up_s).wait_recv()

            @pl.when(k < 4)
            def _():
                ring(ju, up, up_s).start()

        @pl.when(from_above)
        def _():
            ring(jd, down, down_s).wait_recv()

            @pl.when(k < 3)
            def _():
                ring(jd, down, down_s).start()

        @pl.when(from_below)
        def _():
            dy_group(ju)

        @pl.when(from_above)
        def _():
            dy_group(jd)

    def share(t, g):
        part = outs[t].at[g, pl.ds(pl.multiple_of(c * ns, SL), ns)]
        return remote(part, part, sib_s.at[t, g], sib_r.at[t, g], sibling)

    def arrived(t, g):
        part = rows.at[t, g, pl.ds(0, ns - SL)]
        return remote(part, outs[t].at[g, pl.ds(0, ns - SL)], plane_s.at[t, g], plane_r.at[t, g], sibling)

    for t in range(2):

        @pl.loop(0, 4)
        def _(g):
            arrived(t, g).wait_recv()
            row_local(t, g).wait()
            share(t, g).start()

    for t in range(2):

        @pl.loop(0, 4)
        def _(g):
            share(t, g).wait_recv()
            share(t, g).wait_send()
            arrived(t, g).wait_send()

    @pl.when(own)
    def _():
        tab_out.wait_send()

    @pl.when(jnp.logical_not(own))
    def _():
        gout_out.wait_send()

    for i in range(pieces):

        @pl.when(jnp.logical_and(r >= 3, r < 7))
        def _():
            piece(0, i, up).wait_send()

        @pl.when(jnp.logical_or(r == 0, r > 4))
        def _():
            piece(1, i, down).wait_send()

    @pl.loop(0, 4)
    def _(j):
        @pl.when(lax.rem(r - j + 8, 8) < 4)
        def _():
            ring(j, up, up_s).wait_send()

        @pl.when(lax.rem(j - r + 8, 8) < 3)
        def _():
            ring(j, down, down_s).wait_send()


def dispatch(nx, nq, tokens, gout, tabs):
    ntok, width = tokens.shape
    ch = gout.shape[1]
    ns = nq * SL
    hbm = pl.BlockSpec(memory_space=pl.ANY)
    dma = pltpu.SemaphoreType.DMA
    big = jax.ShapeDtypeStruct((4, 2 * ns, 2 * ch), BF)
    return pl.pallas_call(
        functools.partial(dispatch_kernel, nx, nq),
        out_shape=(big, big, jax.ShapeDtypeStruct((2 * nq, ntok), F32)),
        in_specs=[hbm, hbm, hbm],
        out_specs=(hbm, hbm, pl.BlockSpec(memory_space=pltpu.VMEM)),
        scratch_shapes=[
            pltpu.VMEM((4, ntok, 2 * ch), BF),
            pltpu.VMEM((2 * nq, ntok), F32),
            pltpu.VMEM((8, ntok, ch), BF),
            pltpu.VMEM((2, 4, ns, 2 * ch), BF),
            pltpu.VMEM((ns, ntok), BF),
            pltpu.VMEM((ns, 128), F32),
            dma((4,)), dma, dma, dma((2, 4)), dma, dma, dma, dma,
            dma((2, 2 * ROWBLOCKS)), dma((2, 2 * ROWBLOCKS)), dma((4,)), dma((4,)), dma((4,)),
            dma((2, 4)), dma((2, 4)), dma((2, 4)), dma((2, 4)),
        ],
        compiler_params=pltpu.CompilerParams(
            collective_id=1, has_side_effects=True, vmem_limit_bytes=VMEM_LIMIT
        ),
        name="dispatch",
    )(tokens, gout, tabs)


def tdot(a, b):
    return lax.dot_general(a, b, (((0,), (0,)), ((), ())), preferred_element_type=F32)


def dot_t(a, b):
    return lax.dot_general(a, b, (((1,), (1,)), ((), ())), preferred_element_type=F32)


def expert_kernel(x, dy, wg, wu, wd, y, dx, sc, gwg, gwu, gwd):
    groups, _, pair = x.shape

    def total(f):
        acc = f(0)
        for k in range(1, groups):
            acc = acc + f(k)
        return acc

    g = total(lambda k: jnp.dot(x[k], wg[k], preferred_element_type=F32))
    u = total(lambda k: jnp.dot(x[k], wu[k], preferred_element_type=F32))
    sig = jax.nn.sigmoid(g)
    gs = g * sig
    h = (gs * u).astype(BF)
    dh = total(lambda k: dot_t(dy[k], wd[:, k * pair : (k + 1) * pair]))
    dg = (dh * u * sig * (1.0 + g * (1.0 - sig))).astype(BF)
    du = (dh * gs).astype(BF)
    part = h.astype(F32) * dh
    hi = part.astype(BF)
    lo = (part - hi.astype(F32)).astype(BF)
    ones = jnp.ones((8, part.shape[1]), BF)
    sc[...] = (dot_t(ones, hi) + dot_t(ones, lo))[0:1, :]
    for k in range(groups):
        lanes = slice(k * pair, (k + 1) * pair)
        y[k] = jnp.dot(h, wd[:, lanes], preferred_element_type=F32).astype(BF)
        dx[k] = (dot_t(dg, wg[k]) + dot_t(du, wu[k])).astype(BF)
        gwd[:, lanes] = tdot(h, dy[k]).astype(BF)
        gwg[k] = tdot(x[k], dg).astype(BF)
        gwu[k] = tdot(x[k], du).astype(BF)


def expert(x, dy, wg, wu, wd):
    s = jax.ShapeDtypeStruct
    return pl.pallas_call(
        expert_kernel,
        out_shape=(
            s(x.shape, BF), s(x.shape, BF), s((1, x.shape[1]), F32),
            s(wg.shape, BF), s(wu.shape, BF), s(wd.shape, BF),
        ),
        in_specs=[pl.BlockSpec(memory_space=pltpu.VMEM)] * 5,
        out_specs=(pl.BlockSpec(memory_space=pltpu.VMEM),) * 6,
        compiler_params=pltpu.CompilerParams(vmem_limit_bytes=VMEM_LIMIT),
        name="expert",
    )(x, dy, wg, wu, wd)


def combine_kernel(
    nx, nq, y_ref, dx_ref, sc_ref, tab_ref, mixed_ref, gtok_ref, rsc_ref,
    ob, rb, sb, rv, tp, rsd, rsu, fin, fo, wt, scr, st, rsc,
    ob_l, sib_s, sib_r, row_l, plane_s, plane_r, ring_s, down_r, up_r, fin_s, fin_r,
    dp_s, dp_r, ex_s, ex_r,
):
    me, zh, zl, c = place(nx)
    z = zh * 4 + zl
    own = zh == c
    r = lax.rem(z - 4 * c + 8, 8)
    ns = nq * SL
    ntok = tab_ref.shape[1]
    pair = y_ref.shape[2]
    ch = pair // 2
    d = 2 * zl + c
    e = lax.axis_index("expert")
    ne = 2 * nq
    up = device(nx, me, lax.rem(z + 1, 8), c)
    down = device(nx, me, lax.rem(z + 7, 8), c)
    sibling = device(nx, me, z, 1 - c)
    srcs = (y_ref, dx_ref)
    outs = (mixed_ref, gtok_ref)

    barrier = pltpu.get_barrier_semaphore()
    signal(barrier, up)
    signal(barrier, down)

    @pl.loop(1, 8)
    def _(i):
        signal(barrier, {"expert": e, "dp": lax.rem(d + i, 8)})

    @pl.loop(1, ne)
    def _(i):
        signal(barrier, {"expert": lax.rem(e + i, ne), "dp": d})

    pl.semaphore_wait(barrier, 2 + 7 + ne - 1)

    def own_rows(t, g):
        return pltpu.make_async_copy(
            srcs[t].at[g, pl.ds(pl.multiple_of(c * ns, SL), ns)], ob.at[t, g], ob_l.at[t, g]
        )

    def to_sibling(t, g):
        return remote(
            srcs[t].at[g, pl.ds(pl.multiple_of((1 - c) * ns, SL), ns)], rb.at[t, g],
            sib_s.at[t, g], sib_r.at[t, g], sibling,
        )

    scr[pl.ds(d, 1)] = sc_ref[...][None]

    @pl.loop(1, 8)
    def _(i):
        remote(sc_ref, scr.at[d], dp_s, dp_r, {"expert": e, "dp": lax.rem(d + i, 8)}).start()

    for t in range(2):

        @pl.loop(0, 4)
        def _(g):
            own_rows(t, g).start()
            to_sibling(t, g).start()

    rt = tab_ref[0:nq, :]
    gt = tab_ref[nq : 2 * nq, :]
    slot = lax.broadcasted_iota(jnp.int32, (nq, SL, ntok), 1).astype(F32)
    hit = jnp.where(jnp.broadcast_to(rt[:, None, :], (nq, SL, ntok)) == slot, 1.0, 0.0)
    heavy = (hit * jnp.broadcast_to(gt[:, None, :], (nq, SL, ntok))).reshape(ns, ntok).T
    top = heavy.astype(BF)
    wt[0] = top
    wt[1] = (heavy - top.astype(F32)).astype(BF)
    wt[2] = hit.reshape(ns, ntok).T.astype(BF)

    def row_local(t, g):
        rows = pl.ds(pl.multiple_of(me * SL, SL), SL)
        return pltpu.make_async_copy(sb.at[t, g, rows], rv.at[t, g, rows], row_l.at[t, g])

    def arrived(t, g):
        some = pl.ds(0, ns - SL)
        return remote(sb.at[t, g, some], rv.at[t, g, some], plane_s.at[t, g], plane_r.at[t, g], sibling)

    def plane(t, g):
        own_rows(t, g).wait()
        to_sibling(t, g).wait_recv()
        sb[t, g] = (ob[t, g].astype(F32) + rb[t, g].astype(F32)).astype(BF)

        @pl.loop(1, nq)
        def _(i):
            q = lax.rem(me + i, nq)
            remote(
                sb.at[t, g, pl.ds(pl.multiple_of(q * SL, SL), SL)],
                rv.at[t, g, pl.ds(pl.multiple_of(me * SL, SL), SL)],
                plane_s.at[t, g], plane_r.at[t, g], device(nx, q, z, c),
            ).start()

        row_local(t, g).start()

    @pl.loop(0, 4)
    def _(g):
        plane(0, g)

    def all_but_one(a):
        return a.at[pl.ds(0, 7)]

    dp_all = remote(all_but_one(scr), all_but_one(scr), dp_s, dp_r, sibling)
    dp_all.wait_recv()
    st[...] = jnp.sum(scr[...], axis=0)
    rsc[pl.ds(e, 1)] = st[...][None]

    @pl.loop(1, ne)
    def _(i):
        remote(st, rsc.at[e], ex_s, ex_r, {"expert": lax.rem(e + i, ne), "dp": d}).start()

    @pl.loop(0, 4)
    def _(g):
        plane(1, g)

    def send_down(t, j):
        return remote(tp.at[t, j], rsd.at[t, j], ring_s.at[t, j], down_r.at[t, j], down)

    def send_up(t, j):
        return remote(tp.at[t, j], rsu.at[t, j], ring_s.at[t, j], up_r.at[t, j], up)

    for t in range(2):

        @pl.loop(0, 4)
        def _(g):
            arrived(t, g).wait_recv()
            row_local(t, g).wait()
            if t == 0:
                part = jnp.dot(wt[0], rv[t, g], preferred_element_type=F32)
                part = part + jnp.dot(wt[1], rv[t, g], preferred_element_type=F32)
            else:
                part = jnp.dot(wt[2], rv[t, g], preferred_element_type=F32)
            tp[t, g] = part.astype(BF)

            @pl.when(lax.rem(r - g + 8, 8) == 4)
            def _():
                send_down(t, g).start()

            @pl.when(lax.rem(g - r + 8, 8) == 3)
            def _():
                send_up(t, g).start()

        @pl.loop(1, 4)
        def _(n):
            k = 4 - n
            ju = lax.rem(r - k + 8, 8)
            jd = lax.rem(r + k, 8)

            @pl.when(ju < 4)
            def _():
                send_down(t, ju).wait_recv()
                tp[t, ju] = (tp[t, ju].astype(F32) + rsd[t, ju].astype(F32)).astype(BF)
                send_down(t, ju).start()

            @pl.when(jnp.logical_and(jd < 4, k < 3))
            def _():
                send_up(t, jd).wait_recv()
                tp[t, jd] = (tp[t, jd].astype(F32) + rsu[t, jd].astype(F32)).astype(BF)
                send_up(t, jd).start()

        final = remote(fin.at[t], fo.at[t], fin_s.at[t], fin_r.at[t], sibling)

        @pl.when(own)
        def _():
            send_down(t, zl).wait_recv()
            send_up(t, zl).wait_recv()
            whole = tp[t, zl].astype(F32) + rsd[t, zl].astype(F32) + rsu[t, zl].astype(F32)
            low = whole[:, :ch]
            high = pltpu.roll(whole, ch, 1)[:, :ch]
            first = c == 0
            outs[t][...] = jnp.where(first, low, high).astype(BF)
            fin[t] = jnp.where(first, high, low).astype(BF)
            final.start()

    for t in range(2):
        final = remote(fin.at[t], fo.at[t], fin_s.at[t], fin_r.at[t], sibling)

        @pl.when(own)
        def _():
            final.wait_send()

        @pl.when(jnp.logical_not(own))
        def _():
            final.wait_recv()
            outs[t][...] = fo[t]

    some = pl.ds(0, ne - 1)
    ex_all = remote(rsc.at[some], rsc.at[some], ex_s, ex_r, sibling)
    ex_all.wait_recv()
    rsc_ref[...] = rsc[...]
    ex_all.wait_send()
    dp_all.wait_send()
    for t in range(2):

        @pl.loop(0, 4)
        def _(g):
            to_sibling(t, g).wait_send()
            arrived(t, g).wait_send()

            @pl.when(g != r)
            def _():
                send_down(t, g).wait_send()


def combine(nx, nq, ch, ntok, y, dx, sc, tab):
    ns = nq * SL
    pair = 2 * ch
    hbm = pl.BlockSpec(memory_space=pl.ANY)
    vm = pl.BlockSpec(memory_space=pltpu.VMEM)
    dma = pltpu.SemaphoreType.DMA
    s = jax.ShapeDtypeStruct
    wide = pltpu.VMEM((2, 4, ns, pair), BF)
    tall = pltpu.VMEM((2, 4, ntok, pair), BF)
    return pl.pallas_call(
        functools.partial(combine_kernel, nx, nq),
        out_shape=(s((ntok, ch), BF), s((ntok, ch), BF), s((2 * nq, 1, 2 * ns), F32)),
        in_specs=[hbm, hbm, vm, vm],
        out_specs=(vm, vm, vm),
        scratch_shapes=[
            wide, wide, wide, wide, tall, tall, tall,
            pltpu.VMEM((2, ntok, ch), BF), pltpu.VMEM((2, ntok, ch), BF),
            pltpu.VMEM((3, ntok, ns), BF),
            pltpu.VMEM((8, 1, 2 * ns), F32), pltpu.VMEM((1, 2 * ns), F32), pltpu.VMEM((2 * nq, 1, 2 * ns), F32),
            dma((2, 4)), dma((2, 4)), dma((2, 4)), dma((2, 4)), dma((2, 4)), dma((2, 4)),
            dma((2, 4)), dma((2, 4)), dma((2, 4)), dma((2,)), dma((2,)),
            dma, dma, dma, dma,
        ],
        compiler_params=pltpu.CompilerParams(
            collective_id=2, has_side_effects=True, vmem_limit_bytes=VMEM_LIMIT
        ),
        name="combine",
    )(y, dx, sc, tab)


def on_device(nx, tokens, expert_ids, gate_values, tiles, w_gate, w_up, w_down, grad_out):
    ne = lax.axis_size("expert")
    nq = ne // 2
    ntok, width = tokens.shape
    ch = grad_out.shape[1]
    pair = 2 * ch
    live = jnp.arange(ntok, dtype=jnp.int32) < tiles[0] * TILE
    names = jnp.arange(ne, dtype=jnp.int32)[:, None, None]
    chosen = (expert_ids.T[None] == names) & live[None, None, :]
    named = jnp.any(chosen, axis=1)
    earlier = jnp.arange(ntok)[:, None] < jnp.arange(ntok)[None, :]
    rank = jnp.dot(named.astype(BF), earlier.astype(BF), preferred_element_type=F32)
    rank = jnp.where(named, rank, -1.0)
    gate = jnp.sum(jnp.where(chosen, gate_values.T[None], 0.0), axis=1)

    def halves(a):
        return a.reshape(nq // nx, 2, nx, ntok).transpose(1, 0, 2, 3).reshape(2, nq, ntok)

    tabs = jnp.concatenate([halves(rank), halves(gate)], axis=1)
    x, dy, tab = dispatch(nx, nq, tokens, grad_out, tabs)
    fh = w_gate.shape[2]
    wg = w_gate.reshape(4, pair, fh)
    wu = w_up.reshape(4, pair, fh)
    y, dx, sc, gwg, gwu, gwd = expert(x, dy, wg, wu, w_down[0])
    mixed, gtok, rsc = combine(nx, nq, ch, ntok, y, dx, sc, tab)
    e = lax.axis_index("expert")
    zh = (e // nx) % 2
    me = (e // (2 * nx)) * nx + e % nx
    mine = lax.dynamic_slice(rsc[:, 0, :], (0, zh * nq * SL + me * SL), (ne, SL))
    slots = jnp.arange(SL, dtype=F32)
    at = jnp.sum(jnp.where(rank[:, None, :] == slots[None, :, None], mine[:, :, None], 0.0), axis=1)
    at = jnp.where(named, at / jnp.where(named, gate, 1.0), 0.0)
    grad_gates = jnp.sum(jnp.where(chosen, at[:, None, :], 0.0), axis=0).T
    return (
        mixed, gtok, grad_gates,
        gwg.reshape(1, width, fh), gwu.reshape(1, width, fh), gwd[None],
    )


def build(mesh, nx):
    placed = (
        P("expert", None),
        P("expert", None),
        P("expert", None),
        P("expert"),
        P("expert", None, "dp"),
        P("expert", None, "dp"),
        P("expert", "dp", None),
        P("expert", "dp"),
    )
    return jax.shard_map(
        functools.partial(on_device, nx),
        mesh=mesh,
        in_specs=placed,
        out_specs=(
            P("expert", "dp"),
            P("expert", "dp"),
            P("expert", None),
            P("expert", None, "dp"),
            P("expert", None, "dp"),
            P("expert", "dp", None),
        ),
        check_vma=False,
    )


def solution(mesh):
    return build(mesh, 4)
```

time: 482 us -> 378 us (0.78)
  Pallas kernels: 0 us -> 360 us
  blocking collectives: 202 us -> 0 us
  waiting for transfers between devices: 178 us -> 0 us
  matrix products: 50.3 us -> 0.15 us
  between operations: 14.7 us -> 1.39 us
  starting transfers between devices: 13 us -> 0 us
  other arithmetic: 12.9 us -> 3.13 us
    pallas_call x0 -> x3, Pallas kernels: none -> 360 us  [the longest x1 195 us: dispatch(): pl.pallas_call(functools.partial(dispatch_kernel, nx, nq), out_shape=(big...]
    all_to_all x2 -> x0, blocking collectives: 188 us -> none  [the longest x1 114 us: on_device(): lax.all_to_all(dyrow, 'expert', split_axis=0, concat_axis=0, tiled=True)]
    all_gather x1 -> x0, waiting for transfers between devices: 87.7 us -> none  [on_device(): dy_full = lax.all_gather(grad_out, 'dp', axis=1, tiled=True)]
    all_to_all x2 -> x0, waiting for transfers between devices: 78.1 us -> none  [the longest x1 78.1 us: on_device(): lax.all_to_all(input_rows.reshape(experts, SLOTS, width).astype(jnp.bfloa...]
    dot_general x17 -> x1, matrix products: 50.3 us -> 0.15 us  [on_device(): jnp.dot(named.astype(BF), earlier.astype(BF), preferred_element_type=F32)]
    psum x1 -> x0, blocking collectives: 13.3 us -> none  [on_device(): score = lax.psum(jnp.sum(dy_rows * returned, axis=1), 'dp')]
    all_to_all x2 -> x0, starting transfers between devices: 12.9 us -> none  [the longest x1 7.88 us: on_device(): lax.all_to_all(input_rows.reshape(experts, SLOTS, width).astype(jnp.bfloa...]
    reduce_scatter x2 -> x0, waiting for transfers between devices: 11.8 us -> none  [the longest x1 11.8 us: on_device(): lax.psum_scatter(token_grad.astype(jnp.bfloat16), 'dp', scatter_dimension...]
  transfers between devices with their start and end apart: 5 -> 0, of which waited for: 3 -> 0; matrix products, arithmetic and copies ran while one was open for 7% -> 0% of each run, Pallas kernels for 0% -> 0%
where the time goes in v1:
time: 378 us; the launch traced here: 371 us
  Pallas kernels  360 us (95%)
  local copies, waits for them, and re-layouts  6.21 us (2%)
    pallas_call x1, Pallas kernels, dispatch(): pl.pallas_call(functools.partial(dispatch_kernel, nx, nq), out_shape=(big...  195 us
    pallas_call x1, Pallas kernels, combine(): pl.pallas_call(functools.partial(combine_kernel, nx, nq), out_shape=(s((n...  145 us
    pallas_call x1, Pallas kernels, expert(): pl.pallas_call(expert_kernel, out_shape=(s(x.shape, BF), s(x.shape, BF),...  20.3 us

profile of v1, /device:TPU:97, one launch (start us, length us, event | category | flops | bytes accessed | tf_op | source)
XLA Modules:
  0.0 371.0 jit_solution(6758227553066840296)
XLA Ops:
  0.6 1.8 copy.21.gout_ref
  3.1 0.8 select_reduce_fusion.2
  4.0 0.8 fusion.1
  4.8 0.2 convolution_select_fusion
  5.0 0.6 pad_maximum_fusion.tabs_ref
  5.6 194.9 %dispatch.1 = (bf16[4,512,896]{2,1,0:T(8,128)(2,1)}, bf16[4,512,896]{2,1,0:T(8,128)(2,1)}, f32[32,256]{1,0:T(8,128)}) custom-call(bf16[256,3584]{1,0:T(8,128)(2,1)} %tok_ref.1, bf16[256,448]{1,0:T(8,128)(2,1)} %copy.21.gout_ref, f32[2,32,256]{2,1,0:T(8,128)} %pad_maximum_fusion.tabs_ref), custom_call_target="tpu_custom_call" | custom-call | tf_op jit(solution)/shard_map/dispatch/pallas_call | solution.py:283
  200.5 20.3 %expert.1 = (bf16[4,512,896]{2,1,0:T(8,128)(2,1)}, bf16[4,512,896]{2,1,0:T(8,128)(2,1)}, f32[1,512]{1,0:T(1,128)}, bf16[4,896,256]{2,1,0:T(8,128)(2,1)}, bf16[4,...) custom-call(bf16[4,512,896]{2,1,0:T(8,128)(2,1)} %get-tuple-element.18.x, bf16[4,512,896]{2,1,0:T(8,128)(2,1)} %get-tuple-element.19.dy, ...), custom_call_target="tpu_custom_call" | custom-call | tf_op jit(solution)/shard_map/expert/pallas_call | solution.py:347
  220.8 0.0 copy-start
  220.8 145.0 %combine.1 = (bf16[256,448]{1,0:T(8,128)(2,1)}, bf16[256,448]{1,0:T(8,128)(2,1)}, f32[32,1,512]{2,1,0:T(1,128)}) custom-call(bf16[4,512,896]{2,1,0:T(8,128)(2,1)} %get-tuple-element.20.y_ref, bf16[4,512,896]{2,1,0:T(8,128)(2,1)} %get-tuple-element.21.dx_ref, f32[1,512]{1,0:T(1,128)} %get-tuple-element.22.sc_ref, f32[32,256]{1,0:T(8,128)} %get-tuple-element.23.tab_ref), custom_call_target="tpu_custom_call" | custom-call | tf_op jit(solution)/shard_map/combine/pallas_call | solution.py:573
  365.8 1.8 copy.22
  367.6 1.8 copy.23
  369.3 0.8 constant_dynamic-slice_fusion
  370.2 0.2 select_reduce_fusion
  370.4 0.0 copy-done
  370.4 0.7 select_reduce_fusion.1
  (8 shorter events, 0.1 us)
Async XLA Ops:
  220.8 149.6 %copy-start = (s32[256,8]{0,1:T(8,128)S(1)}, s32[256,8]{0,1:T(8,128)}, u32[]{:S(2)}) copy-start(s32[256,8]{0,1:T(8,128)} %param.9) | copy-start | bytes 24580

commit v2 on v1

--- a/solution.py
+++ b/solution.py
@@ -51,7 +51,7 @@
     own = zh == c
     r = lax.rem(z - 4 * c + 8, 8)
     ntok = tok_ref.shape[0]
-    ch = gout_ref.shape[1]
+    ch = gout_ref.shape[0]
     pair = 2 * ch
     ns = nq * SL
     up = device(nx, me, lax.rem(z + 1, 8), c)
@@ -75,17 +75,18 @@
 
     tab_in = pltpu.make_async_copy(tabs_ref.at[zh], tabr, tab_l)
     tab_out = remote(tabs_ref.at[1 - zh], tabr, tab_s, tab_r, across)
-    mine = 2 * zl + c
-    gout_in = pltpu.make_async_copy(gout_ref, dyt.at[mine], gout_l)
-    gout_out = remote(gout_ref, dyt.at[mine], gout_s, gout_r, sibling)
+    mine = dyt.at[zl, pl.ds(pl.multiple_of(c * ch, SL), ch)]
+    gout_in = pltpu.make_async_copy(gout_ref, mine, gout_l)
+    gout_out = remote(gout_ref, mine, gout_s, gout_r, sibling)
 
     def piece(h, i, who):
         step = ntok // ROWBLOCKS
-        part = tok.at[2 * h + i // ROWBLOCKS, pl.ds((i % ROWBLOCKS) * step, step)]
+        first = pl.multiple_of(lax.rem(i, ROWBLOCKS) * step, step)
+        part = tok.at[2 * h + lax.div(i, ROWBLOCKS), pl.ds(first, step)]
         return remote(part, part, x_s.at[h, i], x_r.at[h, i], who)
 
     def ring(j, who, sems):
-        part = dyt.at[pl.ds(2 * j, 2)]
+        part = dyt.at[j]
         return remote(part, part, sems.at[j], ring_r.at[j], who)
 
     pieces = 2 * ROWBLOCKS
@@ -156,10 +157,7 @@
         send_rows(0, g)
 
     def dy_group(g):
-        a = jnp.dot(pick[...], dyt[2 * g], preferred_element_type=F32)
-        b = jnp.dot(pick[...], dyt[2 * g + 1], preferred_element_type=F32)
-        both = jnp.concatenate([a, b], axis=1)
-        rows[1, g] = (both * sg[:, 0:1]).astype(BF)
+        rows[1, g] = (dot_t(pick[...], dyt[g]) * sg[:, 0:1]).astype(BF)
         send_rows(1, g)
 
     @pl.when(own)
@@ -172,22 +170,26 @@
 
     @pl.when(jnp.logical_not(own))
     def _():
-        for i in range(pieces):
-            piece(0, i, up).wait_recv()
-
-            @pl.when(r < 7)
-            def _():
-                piece(0, i, up).start()
-
-            piece(1, i, down).wait_recv()
-
-            @pl.when(r > 4)
-            def _():
-                piece(1, i, down).start()
-
-            if i % ROWBLOCKS == ROWBLOCKS - 1:
-                x_group(i // ROWBLOCKS)
-                x_group(2 + i // ROWBLOCKS)
+        @pl.loop(1, pieces + 4)
+        def _(n):
+            for h, far, who in ((0, r - 3, up), (1, 8 - r, down)):
+                i = n - far
+
+                @pl.when(jnp.logical_and(i >= 0, i < pieces))
+                def _():
+                    piece(h, i, who).wait_recv()
+
+                    @pl.when(far < 4)
+                    def _():
+                        piece(h, i, who).start()
+
+            for h, far in ((0, r - 3), (1, 8 - r)):
+                i = n - far
+                whole = lax.rem(i + ROWBLOCKS, ROWBLOCKS) == ROWBLOCKS - 1
+
+                @pl.when(jnp.logical_and(jnp.logical_and(i >= 0, i < pieces), whole))
+                def _():
+                    x_group(2 * h + lax.div(i, ROWBLOCKS))
 
     @pl.loop(1, 5)
     def _(k):
@@ -275,7 +277,7 @@
 
 def dispatch(nx, nq, tokens, gout, tabs):
     ntok, width = tokens.shape
-    ch = gout.shape[1]
+    ch = gout.shape[0]
     ns = nq * SL
     hbm = pl.BlockSpec(memory_space=pl.ANY)
     dma = pltpu.SemaphoreType.DMA
@@ -288,7 +290,7 @@
         scratch_shapes=[
             pltpu.VMEM((4, ntok, 2 * ch), BF),
             pltpu.VMEM((2 * nq, ntok), F32),
-            pltpu.VMEM((8, ntok, ch), BF),
+            pltpu.VMEM((4, 2 * ch, ntok), BF),
             pltpu.VMEM((2, 4, ns, 2 * ch), BF),
             pltpu.VMEM((ns, ntok), BF),
             pltpu.VMEM((ns, 128), F32),
@@ -422,11 +424,11 @@
     gt = tab_ref[nq : 2 * nq, :]
     slot = lax.broadcasted_iota(jnp.int32, (nq, SL, ntok), 1).astype(F32)
     hit = jnp.where(jnp.broadcast_to(rt[:, None, :], (nq, SL, ntok)) == slot, 1.0, 0.0)
-    heavy = (hit * jnp.broadcast_to(gt[:, None, :], (nq, SL, ntok))).reshape(ns, ntok).T
+    heavy = (hit * jnp.broadcast_to(gt[:, None, :], (nq, SL, ntok))).reshape(ns, ntok)
     top = heavy.astype(BF)
     wt[0] = top
     wt[1] = (heavy - top.astype(F32)).astype(BF)
-    wt[2] = hit.reshape(ns, ntok).T.astype(BF)
+    wt[2] = hit.reshape(ns, ntok).astype(BF)
 
     def row_local(t, g):
         rows = pl.ds(pl.multiple_of(me * SL, SL), SL)
@@ -472,11 +474,18 @@
     def _(g):
         plane(1, g)
 
-    def send_down(t, j):
-        return remote(tp.at[t, j], rsd.at[t, j], ring_s.at[t, j], down_r.at[t, j], down)
-
-    def send_up(t, j):
-        return remote(tp.at[t, j], rsu.at[t, j], ring_s.at[t, j], up_r.at[t, j], up)
+    def half(t, j, n, a):
+        return a.at[t, j, pl.ds(n * ch, ch)]
+
+    def send_down(t, j, n):
+        return remote(half(t, j, n, tp), half(t, j, n, rsd), ring_s.at[t, j, n], down_r.at[t, j, n], down)
+
+    def send_up(t, j, n):
+        return remote(half(t, j, n, tp), half(t, j, n, rsu), ring_s.at[t, j, n], up_r.at[t, j, n], up)
+
+    def add_in(t, j, n, a):
+        both = half(t, j, n, tp)[...].astype(F32) + half(t, j, n, a)[...].astype(F32)
+        half(t, j, n, tp)[...] = both.astype(BF)
 
     for t in range(2):
 
@@ -485,51 +494,56 @@
             arrived(t, g).wait_recv()
             row_local(t, g).wait()
             if t == 0:
-                part = jnp.dot(wt[0], rv[t, g], preferred_element_type=F32)
-                part = part + jnp.dot(wt[1], rv[t, g], preferred_element_type=F32)
+                part = tdot(rv[t, g], wt[0]) + tdot(rv[t, g], wt[1])
             else:
-                part = jnp.dot(wt[2], rv[t, g], preferred_element_type=F32)
+                part = tdot(rv[t, g], wt[2])
             tp[t, g] = part.astype(BF)
 
             @pl.when(lax.rem(r - g + 8, 8) == 4)
             def _():
-                send_down(t, g).start()
+                for n in range(2):
+                    send_down(t, g, n).start()
 
             @pl.when(lax.rem(g - r + 8, 8) == 3)
             def _():
-                send_up(t, g).start()
+                for n in range(2):
+                    send_up(t, g, n).start()
 
         @pl.loop(1, 4)
-        def _(n):
-            k = 4 - n
+        def _(m):
+            k = 4 - m
             ju = lax.rem(r - k + 8, 8)
             jd = lax.rem(r + k, 8)
-
-            @pl.when(ju < 4)
-            def _():
-                send_down(t, ju).wait_recv()
-                tp[t, ju] = (tp[t, ju].astype(F32) + rsd[t, ju].astype(F32)).astype(BF)
-                send_down(t, ju).start()
-
-            @pl.when(jnp.logical_and(jd < 4, k < 3))
-            def _():
-                send_up(t, jd).wait_recv()
-                tp[t, jd] = (tp[t, jd].astype(F32) + rsu[t, jd].astype(F32)).astype(BF)
-                send_up(t, jd).start()
+            for n in range(2):
+
+                @pl.when(ju < 4)
+                def _():
+                    send_down(t, ju, n).wait_recv()
+                    add_in(t, ju, n, rsd)
+                    send_down(t, ju, n).start()
+
+                @pl.when(jnp.logical_and(jd < 4, k < 3))
+                def _():
+                    send_up(t, jd, n).wait_recv()
+                    add_in(t, jd, n, rsu)
+                    send_up(t, jd, n).start()
 
         final = remote(fin.at[t], fo.at[t], fin_s.at[t], fin_r.at[t], sibling)
 
         @pl.when(own)
         def _():
-            send_down(t, zl).wait_recv()
-            send_up(t, zl).wait_recv()
-            whole = tp[t, zl].astype(F32) + rsd[t, zl].astype(F32) + rsu[t, zl].astype(F32)
-            low = whole[:, :ch]
-            high = pltpu.roll(whole, ch, 1)[:, :ch]
-            first = c == 0
-            outs[t][...] = jnp.where(first, low, high).astype(BF)
-            fin[t] = jnp.where(first, high, low).astype(BF)
+            for n in range(2):
+                send_down(t, zl, n).wait_recv()
+                send_up(t, zl, n).wait_recv()
+
+            def summed(core):
+                rows = pl.ds(pl.multiple_of(core * ch, SL), ch)
+                total = tp[t, zl, rows].astype(F32) + rsd[t, zl, rows].astype(F32)
+                return (total + rsu[t, zl, rows].astype(F32)).astype(BF)
+
+            fin[t] = summed(1 - c)
             final.start()
+            outs[t][...] = summed(c)
 
     for t in range(2):
         final = remote(fin.at[t], fo.at[t], fin_s.at[t], fin_r.at[t], sibling)
@@ -558,7 +572,8 @@
 
             @pl.when(g != r)
             def _():
-                send_down(t, g).wait_send()
+                for n in range(2):
+                    send_down(t, g, n).wait_send()
 
 
 def combine(nx, nq, ch, ntok, y, dx, sc, tab):
@@ -569,19 +584,19 @@
     dma = pltpu.SemaphoreType.DMA
     s = jax.ShapeDtypeStruct
     wide = pltpu.VMEM((2, 4, ns, pair), BF)
-    tall = pltpu.VMEM((2, 4, ntok, pair), BF)
+    tall = pltpu.VMEM((2, 4, pair, ntok), BF)
     return pl.pallas_call(
         functools.partial(combine_kernel, nx, nq),
-        out_shape=(s((ntok, ch), BF), s((ntok, ch), BF), s((2 * nq, 1, 2 * ns), F32)),
+        out_shape=(s((ch, ntok), BF), s((ch, ntok), BF), s((2 * nq, 1, 2 * ns), F32)),
         in_specs=[hbm, hbm, vm, vm],
         out_specs=(vm, vm, vm),
         scratch_shapes=[
             wide, wide, wide, wide, tall, tall, tall,
-            pltpu.VMEM((2, ntok, ch), BF), pltpu.VMEM((2, ntok, ch), BF),
-            pltpu.VMEM((3, ntok, ns), BF),
+            pltpu.VMEM((2, ch, ntok), BF), pltpu.VMEM((2, ch, ntok), BF),
+            pltpu.VMEM((3, ns, ntok), BF),
             pltpu.VMEM((8, 1, 2 * ns), F32), pltpu.VMEM((1, 2 * ns), F32), pltpu.VMEM((2 * nq, 1, 2 * ns), F32),
             dma((2, 4)), dma((2, 4)), dma((2, 4)), dma((2, 4)), dma((2, 4)), dma((2, 4)),
-            dma((2, 4)), dma((2, 4)), dma((2, 4)), dma((2,)), dma((2,)),
+            dma((2, 4, 2)), dma((2, 4, 2)), dma((2, 4, 2)), dma((2,)), dma((2,)),
             dma, dma, dma, dma,
         ],
         compiler_params=pltpu.CompilerParams(
@@ -610,7 +625,7 @@
         return a.reshape(nq // nx, 2, nx, ntok).transpose(1, 0, 2, 3).reshape(2, nq, ntok)
 
     tabs = jnp.concatenate([halves(rank), halves(gate)], axis=1)
-    x, dy, tab = dispatch(nx, nq, tokens, grad_out, tabs)
+    x, dy, tab = dispatch(nx, nq, tokens, grad_out.T, tabs)
     fh = w_gate.shape[2]
     wg = w_gate.reshape(4, pair, fh)
     wu = w_up.reshape(4, pair, fh)
@@ -625,7 +640,7 @@
     at = jnp.where(named, at / jnp.where(named, gate, 1.0), 0.0)
     grad_gates = jnp.sum(jnp.where(chosen, at[:, None, :], 0.0), axis=0).T
     return (
-        mixed, gtok, grad_gates,
+        mixed.T, gtok.T, grad_gates,
         gwg.reshape(1, width, fh), gwu.reshape(1, width, fh), gwd[None],
     )
 

time: 378 us -> 206 us (0.54)
  the two profiles are of different devices: /device:TPU:97 before, /device:TPU:99 now
where the time goes in v2:
time: 206 us
  Pallas kernels  197 us (96%)
  local copies, waits for them, and re-layouts  4.17 us (2%)
  other arithmetic  3.13 us (2%)
    pallas_call x1, Pallas kernels, combine(): pl.pallas_call(functools.partial(combine_kernel, nx, nq), out_shape=(s((c...  101 us
    pallas_call x1, Pallas kernels, dispatch(): pl.pallas_call(functools.partial(dispatch_kernel, nx, nq), out_shape=(big...  75.8 us
    pallas_call x1, Pallas kernels, expert(): pl.pallas_call(expert_kernel, out_shape=(s(x.shape, BF), s(x.shape, BF),...  20.3 us

profile of v2, /device:TPU:99, one launch (start us, length us, event | category | flops | bytes accessed | tf_op | source)
XLA Modules:
  0.0 206.0 jit_solution(17775444997605317804)
XLA Ops:
  1.3 0.8 select_reduce_fusion.2
  2.2 0.8 fusion.1
  3.0 0.2 convolution_select_fusion
  3.2 0.6 pad_maximum_fusion.tabs_ref
  3.8 75.8 %dispatch.1 = (bf16[4,512,896]{2,1,0:T(8,128)(2,1)}, bf16[4,512,896]{2,1,0:T(8,128)(2,1)}, f32[32,256]{1,0:T(8,128)}) custom-call(bf16[256,3584]{1,0:T(8,128)(2,1)} %tok_ref.1, bf16[448,256]{1,0:T(8,128)(2,1)} %bitcast.24, f32[2,32,256]{2,1,0:T(8,128)} %pad_maximum_fusion.tabs_ref), custom_call_target="tpu_custom_call" | custom-call | tf_op jit(solution)/shard_map/dispatch/pallas_call | solution.py:285
  79.6 20.3 %expert.1 = (bf16[4,512,896]{2,1,0:T(8,128)(2,1)}, bf16[4,512,896]{2,1,0:T(8,128)(2,1)}, f32[1,512]{1,0:T(1,128)}, bf16[4,896,256]{2,1,0:T(8,128)(2,1)}, bf16[4,...) custom-call(bf16[4,512,896]{2,1,0:T(8,128)(2,1)} %get-tuple-element.18.x, bf16[4,512,896]{2,1,0:T(8,128)(2,1)} %get-tuple-element.19.dy, ...), custom_call_target="tpu_custom_call" | custom-call | tf_op jit(solution)/shard_map/expert/pallas_call | solution.py:349
  99.9 0.0 copy-start
  99.9 101.0 %combine.1 = (bf16[448,256]{1,0:T(8,128)(2,1)}, bf16[448,256]{1,0:T(8,128)(2,1)}, f32[32,1,512]{2,1,0:T(1,128)}) custom-call(bf16[4,512,896]{2,1,0:T(8,128)(2,1)} %get-tuple-element.20.y_ref, bf16[4,512,896]{2,1,0:T(8,128)(2,1)} %get-tuple-element.21.dx_ref, f32[1,512]{1,0:T(1,128)} %get-tuple-element.22.sc_ref, f32[32,256]{1,0:T(8,128)} %get-tuple-element.23.tab_ref), custom_call_target="tpu_custom_call" | custom-call | tf_op jit(solution)/shard_map/combine/pallas_call | solution.py:588
  201.0 0.8 constant_dynamic-slice_fusion
  201.8 0.2 select_reduce_fusion
  202.1 0.0 copy-done
  202.1 0.7 select_reduce_fusion.1
  202.7 1.6 copy.25
  204.4 1.6 copy.26
  (8 shorter events, 0.1 us)
Async XLA Ops:
  99.9 102.2 %copy-start = (s32[256,8]{0,1:T(8,128)S(1)}, s32[256,8]{0,1:T(8,128)}, u32[]{:S(2)}) copy-start(s32[256,8]{0,1:T(8,128)} %param.9) | copy-start | bytes 24580

commit v3 on v0

v3 whole, which is shorter than its diff:
```python
import functools

import jax
import jax.numpy as jnp
from jax import lax
from jax.experimental import pallas as pl
from jax.experimental.pallas import tpu as pltpu
from jax.sharding import PartitionSpec as P

TILE = 128
SL = 16
MESH = pl.DeviceIdType.MESH
VMEM_LIMIT = 60 * 1024 * 1024
BF = jnp.bfloat16
F32 = jnp.float32
ROWBLOCKS = 4
PARTS = 4


def place(nx):
    e = lax.axis_index("expert")
    d = lax.axis_index("dp")
    x = lax.rem(e, nx)
    zh = lax.rem(lax.div(e, nx), 2)
    y = lax.div(e, 2 * nx)
    return y * nx + x, zh, lax.div(d, 2), lax.rem(d, 2)


def device(nx, q, z, core):
    e = (lax.div(q, nx) * 2 + lax.div(z, 4)) * nx + lax.rem(q, nx)
    return {"expert": e, "dp": lax.rem(z, 4) * 2 + core}


def signal(sem, who):
    pl.semaphore_signal(sem, inc=1, device_id=who, device_id_type=MESH)


def remote(src, dst, send, recv, who):
    return pltpu.make_async_remote_copy(
        src_ref=src, dst_ref=dst, send_sem=send, recv_sem=recv, device_id=who, device_id_type=MESH
    )


def tdot(a, b):
    return lax.dot_general(a, b, (((0,), (0,)), ((), ())), preferred_element_type=F32)


def dot_t(a, b):
    return lax.dot_general(a, b, (((1,), (1,)), ((), ())), preferred_element_type=F32)


def moe_kernel(
    nx, nq, tok_ref, gout_ref, tabs_ref, wg_ref, wu_ref, wd_ref,
    mixed_ref, gtok_ref, rsc_ref, gwg_ref, gwu_ref, gwd_ref,
    tok, tabr, dyt, rows, xdy, pick, sg, wt, wg, wu, wd,
    gacc, uacc, dacc, hb, dgb, dub, scb,
    so, ob, rb, rv, tp, rsd, rsu, fin, fo, scr, st, rsc,
    tok_l, tab_l, gout_l, w_l, row_l, back_l, out_l,
    tab_s, tab_r, gout_s, gout_r, x_s, x_r, up_s, down_s, ring_r,
    plane_s, plane_r, share_s, share_r, sib_s, sib_r, back_s, back_r,
    ring_s, down_r, up_r, fin_s, fin_r, dp_s, dp_r, ex_s, ex_r,
):
    me, zh, zl, c = place(nx)
    z = zh * 4 + zl
    e = lax.axis_index("expert")
    d = 2 * zl + c
    own = zh == c
    other = jnp.logical_not(own)
    r = lax.rem(z - 4 * c + 8, 8)
    ntok = tok_ref.shape[0]
    ch = gout_ref.shape[0]
    pair = 2 * ch
    ns = nq * SL
    ne = 2 * nq
    part = pair // PARTS
    up = device(nx, me, lax.rem(z + 1, 8), c)
    down = device(nx, me, lax.rem(z + 7, 8), c)
    across = device(nx, me, lax.rem(z + 4, 8), c)
    sibling = device(nx, me, z, 1 - c)
    outs = (mixed_ref, gtok_ref)
    mine = pl.ds(pl.multiple_of(c * ns, SL), ns)
    theirs = pl.ds(pl.multiple_of((1 - c) * ns, SL), ns)

    def slots(q):
        return pl.ds(pl.multiple_of(q * SL, SL), SL)

    weights = [
        pltpu.make_async_copy(a, b, w_l.at[i])
        for i, (a, b) in enumerate(((wg_ref, wg), (wu_ref, wu), (wd_ref, wd)))
    ]

    def tok_in(g):
        return pltpu.make_async_copy(tok_ref.at[:, pl.ds(g * pair, pair)], tok.at[g], tok_l.at[g])

    tab_in = pltpu.make_async_copy(tabs_ref.at[zh], tabr, tab_l)
    tab_out = remote(tabs_ref.at[1 - zh], tabr, tab_s, tab_r, across)
    chunk = dyt.at[zl, pl.ds(pl.multiple_of(c * ch, SL), ch)]
    gout_in = pltpu.make_async_copy(gout_ref, chunk, gout_l)
    gout_out = remote(gout_ref, chunk, gout_s, gout_r, sibling)

    @pl.when(own)
    def _():
        tab_in.start()
        for g in (0, 2, 1, 3):
            tok_in(g).start()
        gout_in.start()

    for w in weights:
        w.start()

    barrier = pltpu.get_barrier_semaphore()
    signal(barrier, up)
    signal(barrier, down)

    @pl.loop(1, 8)
    def _(i):
        signal(barrier, {"expert": e, "dp": lax.rem(d + i, 8)})

    @pl.loop(1, ne)
    def _(i):
        signal(barrier, {"expert": lax.rem(e + i, ne), "dp": d})

    pl.semaphore_wait(barrier, 2 + 7 + ne - 1)

    def piece(h, i, who):
        step = ntok // ROWBLOCKS
        first = pl.multiple_of(lax.rem(i, ROWBLOCKS) * step, step)
        some = tok.at[2 * h + lax.div(i, ROWBLOCKS), pl.ds(first, step)]
        return remote(some, some, x_s.at[h, i], x_r.at[h, i], who)

    def ring(j, who, sems):
        return remote(dyt.at[j], dyt.at[j], sems.at[j], ring_r.at[j], who)

    pieces = 2 * ROWBLOCKS

    @pl.when(own)
    def _():
        tab_out.start()
        for g in (0, 2, 1, 3):
            tok_in(g).wait()
            for i in range(ROWBLOCKS):
                n = (g % 2) * ROWBLOCKS + i
                if g < 2:

                    @pl.when(r == 3)
                    def _():
                        piece(0, n, up).start()
                else:

                    @pl.when(r == 0)
                    def _():
                        piece(1, n, down).start()

        gout_in.wait()
        gout_out.wait_recv()
        ring(zl, up, up_s).start()
        ring(zl, down, down_s).start()
        tab_in.wait()

    @pl.when(other)
    def _():
        gout_out.start()
        tab_out.wait_recv()

    rt = tabr[0:nq, :]
    gt = tabr[nq : 2 * nq, :]
    slot = lax.broadcasted_iota(jnp.int32, (nq, SL, ntok), 1).astype(F32)
    hit = jnp.where(jnp.broadcast_to(rt[:, None, :], (nq, SL, ntok)) == slot, 1.0, 0.0)
    heavy = (hit * jnp.broadcast_to(gt[:, None, :], (nq, SL, ntok))).reshape(ns, ntok)
    top = heavy.astype(BF)
    pick[...] = hit.reshape(ns, ntok).astype(BF)
    wt[0] = top
    wt[1] = (heavy - top.astype(F32)).astype(BF)
    sg[...] = jnp.broadcast_to(jnp.sum(heavy, axis=1, keepdims=True), sg.shape)

    def row_local(t, g):
        return pltpu.make_async_copy(
            rows.at[t, g, slots(me)], xdy.at[t, g, slots(c * nq + me)], row_l.at[t, g]
        )

    def send_rows(t, g):
        @pl.loop(1, nq)
        def _(i):
            q = lax.rem(me + i, nq)
            remote(
                rows.at[t, g, slots(q)], xdy.at[t, g, slots(c * nq + me)],
                plane_s.at[t, g], plane_r.at[t, g], device(nx, q, z, c),
            ).start()

        row_local(t, g).start()

    def x_group(g):
        rows[0, g] = jnp.dot(pick[...], tok[g], preferred_element_type=F32).astype(BF)
        send_rows(0, g)

    def dy_group(g):
        rows[1, g] = (dot_t(pick[...], dyt[g]) * sg[:, 0:1]).astype(BF)
        send_rows(1, g)

    @pl.when(own)
    def _():
        @pl.loop(0, 4)
        def _(g):
            x_group(g)

        dy_group(zl)

    @pl.when(other)
    def _():
        @pl.loop(1, pieces + 4)
        def _(n):
            for h, far, who in ((0, r - 3, up), (1, 8 - r, down)):
                i = n - far

                @pl.when(jnp.logical_and(i >= 0, i < pieces))
                def _():
                    piece(h, i, who).wait_recv()

                    @pl.when(far < 4)
                    def _():
                        piece(h, i, who).start()

            for h, far in ((0, r - 3), (1, 8 - r)):
                i = n - far
                whole = lax.rem(i + ROWBLOCKS, ROWBLOCKS) == ROWBLOCKS - 1

                @pl.when(jnp.logical_and(jnp.logical_and(i >= 0, i < pieces), whole))
                def _():
                    x_group(2 * h + lax.div(i, ROWBLOCKS))

    @pl.loop(1, 5)
    def _(k):
        ju = lax.rem(r - k + 8, 8)
        jd = lax.rem(r + k, 8)
        from_below = ju < 4
        from_above = jnp.logical_and(jd < 4, k < 4)

        @pl.when(from_below)
        def _():
            ring(ju, up, up_s).wait_recv()

            @pl.when(k < 4)
            def _():
                ring(ju, up, up_s).start()

        @pl.when(from_above)
        def _():
            ring(jd, down, down_s).wait_recv()

            @pl.when(k < 3)
            def _():
                ring(jd, down, down_s).start()

        @pl.when(from_below)
        def _():
            dy_group(ju)

        @pl.when(from_above)
        def _():
            dy_group(jd)

    def share(t, g):
        return remote(xdy.at[t, g, mine], xdy.at[t, g, mine], share_s.at[t, g], share_r.at[t, g], sibling)

    def arrived(t, g):
        some = pl.ds(0, ns - SL)
        return remote(rows.at[t, g, some], xdy.at[t, g, some], plane_s.at[t, g], plane_r.at[t, g], sibling)

    def take_in(t):
        @pl.loop(0, 4)
        def _(g):
            arrived(t, g).wait_recv()
            row_local(t, g).wait()
            share(t, g).start()

    def to_sibling(t, f):
        return remote(so.at[t, f], rb.at[t, f], sib_s.at[t, f], sib_r.at[t, f], sibling)

    def back_local(t, g):
        return pltpu.make_async_copy(ob.at[t, g, slots(me)], rv.at[t, g, slots(me)], back_l.at[t, g])

    def back_arrived(t, g):
        some = pl.ds(0, ns - SL)
        return remote(ob.at[t, g, some], rv.at[t, g, some], back_s.at[t, g], back_r.at[t, g], sibling)

    def send_back(t):
        @pl.loop(0, 4)
        def _(g):
            to_sibling(t, g).wait_recv()
            ob[t, g] = (ob[t, g].astype(F32) + rb[t, g].astype(F32)).astype(BF)

            @pl.loop(1, nq)
            def _(i):
                q = lax.rem(me + i, nq)
                remote(
                    ob.at[t, g, slots(q)], rv.at[t, g, slots(me)],
                    back_s.at[t, g], back_r.at[t, g], device(nx, q, z, c),
                ).start()

            back_local(t, g).start()

    def lanes(f):
        return slice(f * pair, (f + 1) * pair)

    take_in(0)
    weights[0].wait()
    weights[1].wait()
    gacc[...] = jnp.zeros_like(gacc)
    uacc[...] = jnp.zeros_like(uacc)

    @pl.loop(0, 4)
    def _(f):
        share(0, f).wait_recv()
        gacc[...] += jnp.dot(xdy[0, f], wg[f], preferred_element_type=F32)
        uacc[...] += jnp.dot(xdy[0, f], wu[f], preferred_element_type=F32)

    g = gacc[...]
    hb[...] = (g * jax.nn.sigmoid(g) * uacc[...]).astype(BF)
    weights[2].wait()
    for f in range(4):
        so[0, f] = jnp.dot(hb[theirs, :], wd[:, lanes(f)], preferred_element_type=F32).astype(BF)
        to_sibling(0, f).start()
        ob[0, f] = jnp.dot(hb[mine, :], wd[:, lanes(f)], preferred_element_type=F32).astype(BF)

    send_back(0)

    take_in(1)
    dacc[...] = jnp.zeros_like(dacc)
    for f in range(4):
        share(1, f).wait_recv()
        dacc[...] += dot_t(xdy[1, f], wd[:, lanes(f)])

    g = gacc[...]
    u = uacc[...]
    dh = dacc[...]
    sig = jax.nn.sigmoid(g)
    dgb[...] = (dh * u * sig * (1.0 + g * (1.0 - sig))).astype(BF)
    dub[...] = (dh * g * sig).astype(BF)
    prod = hb[...].astype(F32) * dh
    hi = prod.astype(BF)
    lo = (prod - hi.astype(F32)).astype(BF)
    ones = jnp.ones((8, prod.shape[1]), BF)
    scb[...] = (dot_t(ones, hi) + dot_t(ones, lo))[0:1, :]
    scr[pl.ds(d, 1)] = scb[...][None]

    @pl.loop(1, 8)
    def _(i):
        remote(scb, scr.at[d], dp_s, dp_r, {"expert": e, "dp": lax.rem(d + i, 8)}).start()

    @pl.loop(0, 4)
    def _(f):
        so[1, f] = (dot_t(dgb[theirs, :], wg[f]) + dot_t(dub[theirs, :], wu[f])).astype(BF)
        to_sibling(1, f).start()
        ob[1, f] = (dot_t(dgb[mine, :], wg[f]) + dot_t(dub[mine, :], wu[f])).astype(BF)

    send_back(1)

    seven = scr.at[pl.ds(0, 7)]
    dp_all = remote(seven, seven, dp_s, dp_r, sibling)
    dp_all.wait_recv()
    st[...] = jnp.sum(scr[...], axis=0)
    rsc[pl.ds(e, 1)] = st[...][None]

    @pl.loop(1, ne)
    def _(i):
        remote(st, rsc.at[e], ex_s, ex_r, {"expert": lax.rem(e + i, ne), "dp": d}).start()

    @pl.loop(0, 4)
    def _(f):
        wg[f] = tdot(xdy[0, f], dgb[...]).astype(BF)
        wu[f] = tdot(xdy[0, f], dub[...]).astype(BF)

    for f in range(4):
        wd[:, lanes(f)] = tdot(hb[...], xdy[1, f]).astype(BF)

    results = [
        pltpu.make_async_copy(a, b, out_l.at[i])
        for i, (a, b) in enumerate(((wg, gwg_ref), (wu, gwu_ref), (wd, gwd_ref)))
    ]
    for o in results:
        o.start()

    def rows_of(n):
        return pl.ds(pl.multiple_of(n * part, SL), part)

    def send_down(t, j, n):
        return remote(
            tp.at[t, j, rows_of(n)], rsd.at[t, j, rows_of(n)], ring_s.at[t, j, n], down_r.at[t, j, n], down
        )

    def send_up(t, j, n):
        return remote(
            tp.at[t, j, rows_of(n)], rsu.at[t, j, rows_of(n)], ring_s.at[t, j, n], up_r.at[t, j, n], up
        )

    def add_in(t, j, n, a):
        tp[t, j, rows_of(n)] = (
            tp[t, j, rows_of(n)].astype(F32) + a[t, j, rows_of(n)].astype(F32)
        ).astype(BF)

    for t in range(2):

        @pl.loop(0, 4)
        def _(g):
            back_arrived(t, g).wait_recv()
            back_local(t, g).wait()
            if t == 0:
                made = tdot(rv[t, g], wt[0]) + tdot(rv[t, g], wt[1])
            else:
                made = tdot(rv[t, g], pick[...])
            tp[t, g] = made.astype(BF)
            above = lax.rem(r - g + 8, 8)
            below = lax.rem(g - r + 8, 8)

            @pl.when(jnp.logical_and(above > 0, above < 5))
            def _():
                @pl.loop(0, PARTS)
                def _(n):
                    @pl.when(above < 4)
                    def _():
                        send_down(t, g, n).wait_recv()
                        add_in(t, g, n, rsd)

                    send_down(t, g, n).start()

            @pl.when(jnp.logical_and(below > 0, below < 4))
            def _():
                @pl.loop(0, PARTS)
                def _(n):
                    @pl.when(below < 3)
                    def _():
                        send_up(t, g, n).wait_recv()
                        add_in(t, g, n, rsu)

                    send_up(t, g, n).start()

    def final(t):
        return remote(fin.at[t], fo.at[t], fin_s.at[t], fin_r.at[t], sibling)

    @pl.when(own)
    def _():
        for t in range(2):

            @pl.loop(0, PARTS)
            def _(n):
                send_down(t, zl, n).wait_recv()
                send_up(t, zl, n).wait_recv()

            def summed(core):
                some = pl.ds(pl.multiple_of(core * ch, SL), ch)
                total = tp[t, zl, some].astype(F32) + rsd[t, zl, some].astype(F32)
                return (total + rsu[t, zl, some].astype(F32)).astype(BF)

            fin[t] = summed(1 - c)
            final(t).start()
            outs[t][...] = summed(c)

        for t in range(2):
            final(t).wait_send()

        tab_out.wait_send()

    @pl.when(other)
    def _():
        for t in range(2):
            final(t).wait_recv()
            outs[t][...] = fo[t]

        gout_out.wait_send()

    some = pl.ds(0, ne - 1)
    ex_all = remote(rsc.at[some], rsc.at[some], ex_s, ex_r, sibling)
    ex_all.wait_recv()
    rsc_ref[...] = rsc[...]
    ex_all.wait_send()
    dp_all.wait_send()
    for o in results:
        o.wait()

    @pl.loop(0, pieces)
    def _(i):
        @pl.when(jnp.logical_and(r >= 3, r < 7))
        def _():
            piece(0, i, up).wait_send()

        @pl.when(jnp.logical_or(r == 0, r > 4))
        def _():
            piece(1, i, down).wait_send()

    for t in range(2):

        @pl.loop(0, 4)
        def _(g):
            arrived(t, g).wait_send()
            share(t, g).wait_send()
            to_sibling(t, g).wait_send()
            back_arrived(t, g).wait_send()

            @pl.when(g != r)
            def _():
                @pl.loop(0, PARTS)
                def _(n):
                    send_down(t, g, n).wait_send()

    @pl.loop(0, 4)
    def _(j):
        @pl.when(lax.rem(r - j + 8, 8) < 4)
        def _():
            ring(j, up, up_s).wait_send()

        @pl.when(lax.rem(j - r + 8, 8) < 3)
        def _():
            ring(j, down, down_s).wait_send()


def moe(nx, nq, tokens, gout, tabs, wg, wu, wd):
    ntok = tokens.shape[0]
    ch = gout.shape[0]
    pair = 2 * ch
    ns = nq * SL
    fh = wg.shape[2]
    hbm = pl.BlockSpec(memory_space=pl.ANY)
    vm = pl.BlockSpec(memory_space=pltpu.VMEM)
    dma = pltpu.SemaphoreType.DMA
    s = jax.ShapeDtypeStruct
    v = pltpu.VMEM
    wide = v((2, 4, ns, pair), BF)
    tall = v((2, 4, pair, ntok), BF)
    each = dma((2, 4))
    parts = dma((2, 4, PARTS))
    return pl.pallas_call(
        functools.partial(moe_kernel, nx, nq),
        out_shape=(
            s((ch, ntok), BF), s((ch, ntok), BF), s((2 * nq, 1, 2 * ns), F32),
            s(wg.shape, BF), s(wu.shape, BF), s(wd.shape, BF),
        ),
        in_specs=[hbm] * 6,
        out_specs=(vm, vm, vm, hbm, hbm, hbm),
        scratch_shapes=[
            v((4, ntok, pair), BF), v((2 * nq, ntok), F32), v((4, pair, ntok), BF), wide,
            v((2, 4, 2 * ns, pair), BF), v((ns, ntok), BF), v((ns, 128), F32), v((2, ns, ntok), BF),
            v(wg.shape, BF), v(wu.shape, BF), v(wd.shape, BF),
            v((2 * ns, fh), F32), v((2 * ns, fh), F32), v((2 * ns, fh), F32),
            v((2 * ns, fh), BF), v((2 * ns, fh), BF), v((2 * ns, fh), BF), v((1, 2 * ns), F32),
            wide, wide, wide, wide, tall, tall, tall, v((2, ch, ntok), BF), v((2, ch, ntok), BF),
            v((8, 1, 2 * ns), F32), v((1, 2 * ns), F32), v((2 * nq, 1, 2 * ns), F32),
            dma((4,)), dma, dma, dma((3,)), each, each, dma((3,)),
            dma, dma, dma, dma, dma((2, 2 * ROWBLOCKS)), dma((2, 2 * ROWBLOCKS)), dma((4,)), dma((4,)), dma((4,)),
            each, each, each, each, each, each, each, each,
            parts, parts, parts, dma((2,)), dma((2,)), dma, dma, dma, dma,
        ],
        compiler_params=pltpu.CompilerParams(
            collective_id=1, has_side_effects=True, vmem_limit_bytes=VMEM_LIMIT
        ),
        name="moe",
    )(tokens, gout, tabs, wg, wu, wd)


def on_device(nx, tokens, expert_ids, gate_values, tiles, w_gate, w_up, w_down, grad_out):
    ne = lax.axis_size("expert")
    nq = ne // 2
    ntok, width = tokens.shape
    ch = grad_out.shape[1]
    pair = 2 * ch
    live = jnp.arange(ntok, dtype=jnp.int32) < tiles[0] * TILE
    names = jnp.arange(ne, dtype=jnp.int32)[:, None, None]
    chosen = (expert_ids.T[None] == names) & live[None, None, :]
    named = jnp.any(chosen, axis=1)
    earlier = jnp.arange(ntok)[:, None] < jnp.arange(ntok)[None, :]
    rank = jnp.dot(named.astype(BF), earlier.astype(BF), preferred_element_type=F32)
    rank = jnp.where(named, rank, -1.0)
    gate = jnp.sum(jnp.where(chosen, gate_values.T[None], 0.0), axis=1)

    def halves(a):
        return a.reshape(nq // nx, 2, nx, ntok).transpose(1, 0, 2, 3).reshape(2, nq, ntok)

    tabs = jnp.concatenate([halves(rank), halves(gate)], axis=1)
    fh = w_gate.shape[2]
    wg = w_gate.reshape(4, pair, fh)
    wu = w_up.reshape(4, pair, fh)
    mixed, gtok, rsc, gwg, gwu, gwd = moe(nx, nq, tokens, grad_out.T, tabs, wg, wu, w_down[0])
    e = lax.axis_index("expert")
    zh = (e // nx) % 2
    me = (e // (2 * nx)) * nx + e % nx
    mine = lax.dynamic_slice(rsc[:, 0, :], (0, zh * nq * SL + me * SL), (ne, SL))
    slots = jnp.arange(SL, dtype=F32)
    at = jnp.sum(jnp.where(rank[:, None, :] == slots[None, :, None], mine[:, :, None], 0.0), axis=1)
    at = jnp.where(named, at / jnp.where(named, gate, 1.0), 0.0)
    grad_gates = jnp.sum(jnp.where(chosen, at[:, None, :], 0.0), axis=0).T
    return (
        mixed.T, gtok.T, grad_gates,
        gwg.reshape(1, width, fh), gwu.reshape(1, width, fh), gwd[None],
    )


def build(mesh, nx):
    placed = (
        P("expert", None),
        P("expert", None),
        P("expert", None),
        P("expert"),
        P("expert", None, "dp"),
        P("expert", None, "dp"),
        P("expert", "dp", None),
        P("expert", "dp"),
    )
    return jax.shard_map(
        functools.partial(on_device, nx),
        mesh=mesh,
        in_specs=placed,
        out_specs=(
            P("expert", "dp"),
            P("expert", "dp"),
            P("expert", None),
            P("expert", None, "dp"),
            P("expert", None, "dp"),
            P("expert", "dp", None),
        ),
        check_vma=False,
    )


def solution(mesh):
    return build(mesh, 4)
```

time: 482 us -> 189 us (0.39)
  blocking collectives: 202 us -> 0 us
  waiting for transfers between devices: 178 us -> 0 us
  Pallas kernels: 0 us -> 174 us
  matrix products: 50.3 us -> 0.15 us
  between operations: 14.7 us -> 1.42 us
  starting transfers between devices: 13 us -> 0 us
  other arithmetic: 12.9 us -> 3.14 us
    all_to_all x2 -> x0, blocking collectives: 188 us -> none  [the longest x1 114 us: on_device(): lax.all_to_all(dyrow, 'expert', split_axis=0, concat_axis=0, tiled=True)]
    pallas_call x0 -> x1, Pallas kernels: none -> 174 us  [moe(): pl.pallas_call(functools.partial(moe_kernel, nx, nq), out_shape=(s((ch, n...]
    all_gather x1 -> x0, waiting for transfers between devices: 87.7 us -> none  [on_device(): dy_full = lax.all_gather(grad_out, 'dp', axis=1, tiled=True)]
    all_to_all x2 -> x0, waiting for transfers between devices: 78.1 us -> none  [the longest x1 78.1 us: on_device(): lax.all_to_all(input_rows.reshape(experts, SLOTS, width).astype(jnp.bfloa...]
    dot_general x17 -> x1, matrix products: 50.3 us -> 0.15 us  [on_device(): jnp.dot(named.astype(BF), earlier.astype(BF), preferred_element_type=F32)]
    psum x1 -> x0, blocking collectives: 13.3 us -> none  [on_device(): score = lax.psum(jnp.sum(dy_rows * returned, axis=1), 'dp')]
    all_to_all x2 -> x0, starting transfers between devices: 12.9 us -> none  [the longest x1 7.88 us: on_device(): lax.all_to_all(input_rows.reshape(experts, SLOTS, width).astype(jnp.bfloa...]
    reduce_scatter x2 -> x0, waiting for transfers between devices: 11.8 us -> none  [the longest x1 11.8 us: on_device(): lax.psum_scatter(token_grad.astype(jnp.bfloat16), 'dp', scatter_dimension...]
  transfers between devices with their start and end apart: 5 -> 0, of which waited for: 3 -> 0; matrix products, arithmetic and copies ran while one was open for 7% -> 0% of each run, Pallas kernels for 0% -> 0%
where the time goes in v3:
time: 189 us
  Pallas kernels  174 us (92%)
  local copies, waits for them, and re-layouts  10.5 us (6%)
  other arithmetic  3.14 us (2%)
    pallas_call x1, Pallas kernels, moe(): pl.pallas_call(functools.partial(moe_kernel, nx, nq), out_shape=(s((ch, n...  174 us
    unnamed x11, local copies, waits for them, and re-layouts  9.66 us

profile of v3, /device:TPU:97, one launch (start us, length us, event | category | flops | bytes accessed | tf_op | source)
XLA Modules:
  0.0 188.9 jit_solution(8018274092342150704)
XLA Ops:
  1.3 0.8 fusion.1
  2.1 0.2 convolution_select_fusion
  2.3 0.8 select_reduce_fusion.2
  3.2 0.6 pad_maximum_fusion.tabs_ref
  3.9 0.0 copy-start.2
  3.9 173.7 %moe.1 = (bf16[448,256]{1,0:T(8,128)(2,1)}, bf16[448,256]{1,0:T(8,128)(2,1)}, f32[32,1,512]{2,1,0:T(1,128)}, bf16[4,896,256]{2,1,0:T(8,128)(2,1)}, bf16[4,896,25...) custom-call(bf16[256,3584]{1,0:T(8,128)(2,1)} %tok_ref.1, bf16[448,256]{1,0:T(8,128)(2,1)} %bitcast.29, ...), custom_call_target="tpu_custom_call" | custom-call | tf_op jit(solution)/shard_map/moe/pallas_call | solution.py:531
  177.6 0.8 constant_dynamic-slice_fusion
  178.4 0.2 select_reduce_fusion
  178.6 0.0 copy-done.2
  178.6 0.7 select_reduce_fusion.1
  179.3 1.6 copy.28
  180.9 1.6 copy.29
  182.6 0.0 copy-start.1
  182.6 3.0 %copy.30 = bf16[1,3584,256]{2,1,0:T(8,128)(2,1)} copy(bf16[1,3584,256]{2,1,0:T(8,128)(2,1)} %bitcast.23) | data formatting | bytes 3670016
  185.5 0.0 copy-done.1
  185.5 0.0 copy-start
  185.6 1.2 copy.31
  186.8 0.9 copy-done
  187.7 1.2 copy.32
  (8 shorter events, 0.1 us)
Async XLA Ops:
  3.9 174.8 %copy-start.2 = (s32[256,8]{0,1:T(8,128)S(1)}, s32[256,8]{0,1:T(8,128)}, u32[]{:S(2)}) copy-start(s32[256,8]{0,1:T(8,128)} %param.9) | copy-start | bytes 24580
  182.6 3.0 %copy-start.1 = (bf16[4,896,256]{2,1,0:T(8,128)(2,1)S(1)}, bf16[4,896,256]{2,1,0:T(8,128)(2,1)}, u32[]{:S(2)}) copy-start(bf16[4,896,256]{2,1,0:T(8,128)(2,1)} %get-tuple-element.16) | copy-start | bytes 5505028
  185.5 2.2 %copy-start = (bf16[256,3584]{1,0:T(8,128)(2,1)S(1)}, bf16[256,3584]{1,0:T(8,128)(2,1)}, u32[]{:S(2)}) copy-start(bf16[256,3584]{1,0:T(8,128)(2,1)} %get-tuple-element.17) | copy-start | bytes 5505028

commit v4 on v3

--- a/solution.py
+++ b/solution.py
@@ -15,6 +15,10 @@
 F32 = jnp.float32
 ROWBLOCKS = 4
 PARTS = 4
+SKEW = 2
+RING_FIRST = 9
+RING_STEP = 4
+RING_INSIDE = 2
 
 
 def place(nx):
@@ -197,39 +201,7 @@
         rows[1, g] = (dot_t(pick[...], dyt[g]) * sg[:, 0:1]).astype(BF)
         send_rows(1, g)
 
-    @pl.when(own)
-    def _():
-        @pl.loop(0, 4)
-        def _(g):
-            x_group(g)
-
-        dy_group(zl)
-
-    @pl.when(other)
-    def _():
-        @pl.loop(1, pieces + 4)
-        def _(n):
-            for h, far, who in ((0, r - 3, up), (1, 8 - r, down)):
-                i = n - far
-
-                @pl.when(jnp.logical_and(i >= 0, i < pieces))
-                def _():
-                    piece(h, i, who).wait_recv()
-
-                    @pl.when(far < 4)
-                    def _():
-                        piece(h, i, who).start()
-
-            for h, far in ((0, r - 3), (1, 8 - r)):
-                i = n - far
-                whole = lax.rem(i + ROWBLOCKS, ROWBLOCKS) == ROWBLOCKS - 1
-
-                @pl.when(jnp.logical_and(jnp.logical_and(i >= 0, i < pieces), whole))
-                def _():
-                    x_group(2 * h + lax.div(i, ROWBLOCKS))
-
-    @pl.loop(1, 5)
-    def _(k):
+    def ring_step(k):
         ju = lax.rem(r - k + 8, 8)
         jd = lax.rem(r + k, 8)
         from_below = ju < 4
@@ -258,6 +230,54 @@
         @pl.when(from_above)
         def _():
             dy_group(jd)
+
+    @pl.when(own)
+    def _():
+        @pl.loop(0, 4)
+        def _(g):
+            x_group(g)
+
+        dy_group(zl)
+
+    @pl.when(other)
+    def _():
+        @pl.loop(SKEW, pieces + 4 * SKEW)
+        def _(n):
+            for h, far, who in ((0, r - 3, up), (1, 8 - r, down)):
+                i = n - far * SKEW
+
+                @pl.when(jnp.logical_and(i >= 0, i < pieces))
+                def _():
+                    piece(h, i, who).wait_recv()
+
+                    @pl.when(far < 4)
+                    def _():
+                        piece(h, i, who).start()
+
+            for h, far in ((0, r - 3), (1, 8 - r)):
+                i = n - far * SKEW
+                whole = lax.rem(i + 4 * ROWBLOCKS, ROWBLOCKS) == ROWBLOCKS - 1
+
+                @pl.when(jnp.logical_and(jnp.logical_and(i >= 0, i < pieces), whole))
+                def _():
+                    x_group(2 * h + lax.div(i, ROWBLOCKS))
+
+            k = lax.div(n - RING_FIRST, RING_STEP) + 1
+            turn = lax.rem(n - RING_FIRST + RING_STEP * 8, RING_STEP) == 0
+
+            @pl.when(jnp.logical_and(jnp.logical_and(n >= RING_FIRST, k <= RING_INSIDE), turn))
+            def _():
+                ring_step(k)
+
+        @pl.loop(RING_INSIDE + 1, 5)
+        def _(k):
+            ring_step(k)
+
+    @pl.when(own)
+    def _():
+        @pl.loop(1, 4)
+        def _(k):
+            ring_step(k)
 
     def share(t, g):
         return remote(xdy.at[t, g, mine], xdy.at[t, g, mine], share_s.at[t, g], share_r.at[t, g], sibling)
@@ -398,41 +418,55 @@
             tp[t, j, rows_of(n)].astype(F32) + a[t, j, rows_of(n)].astype(F32)
         ).astype(BF)
 
-    for t in range(2):
-
-        @pl.loop(0, 4)
-        def _(g):
+    def pass_on(t, g, m):
+        above = lax.rem(r - g + 8, 8)
+        below = lax.rem(g - r + 8, 8)
+
+        @pl.when(above == 4 - m)
+        def _():
+            @pl.loop(0, PARTS)
+            def _(n):
+                if m > 0:
+                    send_down(t, g, n).wait_recv()
+                    add_in(t, g, n, rsd)
+                send_down(t, g, n).start()
+
+        if m < 3:
+
+            @pl.when(below == 3 - m)
+            def _():
+                @pl.loop(0, PARTS)
+                def _(n):
+                    if m > 0:
+                        send_up(t, g, n).wait_recv()
+                        add_in(t, g, n, rsu)
+                    send_up(t, g, n).start()
+
+    @pl.loop(0, 11)
+    def _(n):
+        for m in (3, 2, 1):
+            at = n - m
+
+            @pl.when(jnp.logical_and(at >= 0, at < 8))
+            def _():
+                pass_on(lax.div(at, 4), lax.rem(at, 4), m)
+
+        @pl.when(n < 8)
+        def _():
+            t = lax.div(n, 4)
+            g = lax.rem(n, 4)
             back_arrived(t, g).wait_recv()
             back_local(t, g).wait()
-            if t == 0:
-                made = tdot(rv[t, g], wt[0]) + tdot(rv[t, g], wt[1])
-            else:
-                made = tdot(rv[t, g], pick[...])
-            tp[t, g] = made.astype(BF)
-            above = lax.rem(r - g + 8, 8)
-            below = lax.rem(g - r + 8, 8)
-
-            @pl.when(jnp.logical_and(above > 0, above < 5))
-            def _():
-                @pl.loop(0, PARTS)
-                def _(n):
-                    @pl.when(above < 4)
-                    def _():
-                        send_down(t, g, n).wait_recv()
-                        add_in(t, g, n, rsd)
-
-                    send_down(t, g, n).start()
-
-            @pl.when(jnp.logical_and(below > 0, below < 4))
-            def _():
-                @pl.loop(0, PARTS)
-                def _(n):
-                    @pl.when(below < 3)
-                    def _():
-                        send_up(t, g, n).wait_recv()
-                        add_in(t, g, n, rsu)
-
-                    send_up(t, g, n).start()
+
+            @pl.when(t == 0)
+            def _():
+                tp[0, g] = (tdot(rv[0, g], wt[0]) + tdot(rv[0, g], wt[1])).astype(BF)
+
+            @pl.when(t == 1)
+            def _():
+                tp[1, g] = tdot(rv[1, g], pick[...]).astype(BF)
+
+            pass_on(t, g, 0)
 
     def final(t):
         return remote(fin.at[t], fo.at[t], fin_s.at[t], fin_r.at[t], sibling)

time: 189 us -> 170 us (0.90)
  Pallas kernels: 174 us -> 154 us
    pallas_call x1, Pallas kernels: 174 us -> 154 us  [moe(): pl.pallas_call(functools.partial(moe_kernel, nx, nq), out_shape=(s((ch, n...]
where the time goes in v4:
time: 170 us
  Pallas kernels  154 us (91%)
  local copies, waits for them, and re-layouts  10.5 us (6%)
  other arithmetic  3.14 us (2%)
    pallas_call x1, Pallas kernels, moe(): pl.pallas_call(functools.partial(moe_kernel, nx, nq), out_shape=(s((ch, n...  154 us
    unnamed x11, local copies, waits for them, and re-layouts  9.66 us

profile of v4, /device:TPU:97, one launch (start us, length us, event | category | flops | bytes accessed | tf_op | source)
XLA Modules:
  0.0 169.7 jit_solution(1415957487636833831)
XLA Ops:
  1.3 0.8 fusion.1
  2.1 0.2 convolution_select_fusion
  2.3 0.8 select_reduce_fusion.2
  3.2 0.6 pad_maximum_fusion.tabs_ref
  3.9 0.0 copy-start.2
  3.9 154.4 %moe.1 = (bf16[448,256]{1,0:T(8,128)(2,1)}, bf16[448,256]{1,0:T(8,128)(2,1)}, f32[32,1,512]{2,1,0:T(1,128)}, bf16[4,896,256]{2,1,0:T(8,128)(2,1)}, bf16[4,896,25...) custom-call(bf16[256,3584]{1,0:T(8,128)(2,1)} %tok_ref.1, bf16[448,256]{1,0:T(8,128)(2,1)} %bitcast.29, ...), custom_call_target="tpu_custom_call" | custom-call | tf_op jit(solution)/shard_map/moe/pallas_call | solution.py:565
  158.3 0.8 constant_dynamic-slice_fusion
  159.1 0.2 select_reduce_fusion
  159.4 0.0 copy-done.2
  159.4 0.7 select_reduce_fusion.1
  160.0 1.6 copy.28
  161.7 1.6 copy.29
  163.3 0.0 copy-start.1
  163.3 3.0 %copy.30 = bf16[1,3584,256]{2,1,0:T(8,128)(2,1)} copy(bf16[1,3584,256]{2,1,0:T(8,128)(2,1)} %bitcast.23) | data formatting | bytes 3670016
  166.3 0.0 copy-done.1
  166.3 0.0 copy-start
  166.3 1.2 copy.31
  167.5 0.9 copy-done
  168.5 1.2 copy.32
  (8 shorter events, 0.1 us)
Async XLA Ops:
  3.9 155.5 %copy-start.2 = (s32[256,8]{0,1:T(8,128)S(1)}, s32[256,8]{0,1:T(8,128)}, u32[]{:S(2)}) copy-start(s32[256,8]{0,1:T(8,128)} %param.9) | copy-start | bytes 24580
  163.3 3.0 %copy-start.1 = (bf16[4,896,256]{2,1,0:T(8,128)(2,1)S(1)}, bf16[4,896,256]{2,1,0:T(8,128)(2,1)}, u32[]{:S(2)}) copy-start(bf16[4,896,256]{2,1,0:T(8,128)(2,1)} %get-tuple-element.16) | copy-start | bytes 5505028
  166.3 2.2 %copy-start = (bf16[256,3584]{1,0:T(8,128)(2,1)S(1)}, bf16[256,3584]{1,0:T(8,128)(2,1)}, u32[]{:S(2)}) copy-start(bf16[256,3584]{1,0:T(8,128)(2,1)} %get-tuple-element.17) | copy-start | bytes 5505028

commit v5 on v4

--- a/solution.py
+++ b/solution.py
@@ -15,10 +15,8 @@
 F32 = jnp.float32
 ROWBLOCKS = 4
 PARTS = 4
-SKEW = 2
-RING_FIRST = 9
-RING_STEP = 4
-RING_INSIDE = 2
+SKEW = 3
+RING_FIRST = 6
 
 
 def place(nx):
@@ -53,13 +51,31 @@
     return lax.dot_general(a, b, (((1,), (1,)), ((), ())), preferred_element_type=F32)
 
 
+def routing(ids, gates, tiles, names):
+    top, ntok = ids.shape
+    named = names < 0
+    gate = jnp.zeros((names.shape[0], ntok), F32)
+    named = jnp.broadcast_to(named, gate.shape)
+    for k in range(top):
+        chosen = ids[k : k + 1, :] == names
+        named = jnp.logical_or(named, chosen)
+        gate = gate + jnp.where(chosen, gates[k : k + 1, :], 0.0)
+    live = lax.broadcasted_iota(jnp.int32, gate.shape, 1) < tiles * TILE
+    named = jnp.logical_and(named, live)
+    square = (ntok, ntok)
+    earlier = lax.broadcasted_iota(jnp.int32, square, 0) < lax.broadcasted_iota(jnp.int32, square, 1)
+    ones = jnp.where(named, 1.0, 0.0).astype(BF)
+    before = jnp.dot(ones, jnp.where(earlier, 1.0, 0.0).astype(BF), preferred_element_type=F32)
+    return jnp.where(named, before, -1.0), gate
+
+
 def moe_kernel(
-    nx, nq, tok_ref, gout_ref, tabs_ref, wg_ref, wu_ref, wd_ref,
+    nx, nq, tok_ref, gout_ref, ids_ref, gates_ref, tiles_ref, wg_ref, wu_ref, wd_ref,
     mixed_ref, gtok_ref, rsc_ref, gwg_ref, gwu_ref, gwd_ref,
-    tok, tabr, dyt, rows, xdy, pick, sg, wt, wg, wu, wd,
+    tok, tabs, tabr, dyt, rows, xdy, pick, sg, wt, wg, wu, wd,
     gacc, uacc, dacc, hb, dgb, dub, scb,
     so, ob, rb, rv, tp, rsd, rsu, fin, fo, scr, st, rsc,
-    tok_l, tab_l, gout_l, w_l, row_l, back_l, out_l,
+    tok_l, gout_l, w_l, row_l, back_l, out_l,
     tab_s, tab_r, gout_s, gout_r, x_s, x_r, up_s, down_s, ring_r,
     plane_s, plane_r, share_s, share_r, sib_s, sib_r, back_s, back_r,
     ring_s, down_r, up_r, fin_s, fin_r, dp_s, dp_r, ex_s, ex_r,
@@ -96,15 +112,13 @@
     def tok_in(g):
         return pltpu.make_async_copy(tok_ref.at[:, pl.ds(g * pair, pair)], tok.at[g], tok_l.at[g])
 
-    tab_in = pltpu.make_async_copy(tabs_ref.at[zh], tabr, tab_l)
-    tab_out = remote(tabs_ref.at[1 - zh], tabr, tab_s, tab_r, across)
+    tab_out = remote(tabs.at[1 - zh], tabr, tab_s, tab_r, across)
     chunk = dyt.at[zl, pl.ds(pl.multiple_of(c * ch, SL), ch)]
     gout_in = pltpu.make_async_copy(gout_ref, chunk, gout_l)
     gout_out = remote(gout_ref, chunk, gout_s, gout_r, sibling)
 
     @pl.when(own)
     def _():
-        tab_in.start()
         for g in (0, 2, 1, 3):
             tok_in(g).start()
         gout_in.start()
@@ -123,6 +137,18 @@
     @pl.loop(1, ne)
     def _(i):
         signal(barrier, {"expert": lax.rem(e + i, ne), "dp": d})
+
+    row = lax.broadcasted_iota(jnp.int32, (nq, 1), 0)
+    shift = nx.bit_length() - 1
+    for h in range(2):
+        names = lax.shift_right_logical(row, shift) * (2 * nx) + h * nx + jnp.bitwise_and(row, nx - 1)
+        rank, gate = routing(ids_ref[...], gates_ref[...], tiles_ref[0:1, 0:1], names)
+        tabs[h, 0:nq] = rank
+        tabs[h, nq : 2 * nq] = gate
+
+    @pl.when(own)
+    def _():
+        tabr[...] = tabs[zh]
 
     pl.semaphore_wait(barrier, 2 + 7 + ne - 1)
 
@@ -132,8 +158,9 @@
         some = tok.at[2 * h + lax.div(i, ROWBLOCKS), pl.ds(first, step)]
         return remote(some, some, x_s.at[h, i], x_r.at[h, i], who)
 
-    def ring(j, who, sems):
-        return remote(dyt.at[j], dyt.at[j], sems.at[j], ring_r.at[j], who)
+    def ring(j, n, who, sems):
+        some = dyt.at[j, pl.ds(pl.multiple_of(n * ch, SL), ch)]
+        return remote(some, some, sems.at[j, n], ring_r.at[j, n], who)
 
     pieces = 2 * ROWBLOCKS
 
@@ -156,10 +183,11 @@
                         piece(1, n, down).start()
 
         gout_in.wait()
+        ring(zl, c, up, up_s).start()
+        ring(zl, c, down, down_s).start()
         gout_out.wait_recv()
-        ring(zl, up, up_s).start()
-        ring(zl, down, down_s).start()
-        tab_in.wait()
+        ring(zl, 1 - c, up, up_s).start()
+        ring(zl, 1 - c, down, down_s).start()
 
     @pl.when(other)
     def _():
@@ -201,7 +229,8 @@
         rows[1, g] = (dot_t(pick[...], dyt[g]) * sg[:, 0:1]).astype(BF)
         send_rows(1, g)
 
-    def ring_step(k):
+    def ring_step(k, m):
+        n = lax.rem(c + m, 2)
         ju = lax.rem(r - k + 8, 8)
         jd = lax.rem(r + k, 8)
         from_below = ju < 4
@@ -209,35 +238,51 @@
 
         @pl.when(from_below)
         def _():
-            ring(ju, up, up_s).wait_recv()
+            ring(ju, n, up, up_s).wait_recv()
 
             @pl.when(k < 4)
             def _():
-                ring(ju, up, up_s).start()
+                ring(ju, n, up, up_s).start()
 
         @pl.when(from_above)
         def _():
-            ring(jd, down, down_s).wait_recv()
+            ring(jd, n, down, down_s).wait_recv()
 
             @pl.when(k < 3)
             def _():
-                ring(jd, down, down_s).start()
-
-        @pl.when(from_below)
+                ring(jd, n, down, down_s).start()
+
+        @pl.when(jnp.logical_and(from_below, m == 1))
         def _():
             dy_group(ju)
 
-        @pl.when(from_above)
+        @pl.when(jnp.logical_and(from_above, m == 1))
         def _():
             dy_group(jd)
 
     @pl.when(own)
     def _():
-        @pl.loop(0, 4)
-        def _(g):
-            x_group(g)
-
-        dy_group(zl)
+        @pl.loop(0, 11)
+        def _(n):
+            @pl.when(n < 2)
+            def _():
+                x_group(n)
+
+            @pl.when(jnp.logical_and(n > 3, n < 6))
+            def _():
+                x_group(n - 2)
+
+            @pl.when(n == 6)
+            def _():
+                dy_group(zl)
+
+            @pl.when(jnp.logical_and(n > 1, n < 4))
+            def _():
+                ring_step(1, n - 2)
+
+            @pl.when(n > 6)
+            def _():
+                ring_step(2 + lax.div(n - 7, 2), lax.rem(n - 7, 2))
 
     @pl.when(other)
     def _():
@@ -262,22 +307,13 @@
                 def _():
                     x_group(2 * h + lax.div(i, ROWBLOCKS))
 
-            k = lax.div(n - RING_FIRST, RING_STEP) + 1
-            turn = lax.rem(n - RING_FIRST + RING_STEP * 8, RING_STEP) == 0
-
-            @pl.when(jnp.logical_and(jnp.logical_and(n >= RING_FIRST, k <= RING_INSIDE), turn))
-            def _():
-                ring_step(k)
-
-        @pl.loop(RING_INSIDE + 1, 5)
-        def _(k):
-            ring_step(k)
-
-    @pl.when(own)
-    def _():
-        @pl.loop(1, 4)
-        def _(k):
-            ring_step(k)
+            at = n - RING_FIRST
+
+            @pl.when(jnp.logical_and(at >= 0, lax.rem(at + 8, 2) == 0))
+            def _():
+                ring_step(lax.div(at, 4) + 1, lax.div(lax.rem(at, 4), 2))
+
+        ring_step(4, 1)
 
     def share(t, g):
         return remote(xdy.at[t, g, mine], xdy.at[t, g, mine], share_s.at[t, g], share_r.at[t, g], sibling)
@@ -442,6 +478,24 @@
                         add_in(t, g, n, rsu)
                     send_up(t, g, n).start()
 
+    def final(t):
+        return remote(fin.at[t], fo.at[t], fin_s.at[t], fin_r.at[t], sibling)
+
+    def finish_own(t):
+        @pl.loop(0, PARTS)
+        def _(n):
+            send_down(t, zl, n).wait_recv()
+            send_up(t, zl, n).wait_recv()
+
+        def summed(core):
+            some = pl.ds(pl.multiple_of(core * ch, SL), ch)
+            total = tp[t, zl, some].astype(F32) + rsd[t, zl, some].astype(F32)
+            return (total + rsu[t, zl, some].astype(F32)).astype(BF)
+
+        fin[t] = summed(1 - c)
+        final(t).start()
+        outs[t][...] = summed(c)
+
     @pl.loop(0, 11)
     def _(n):
         for m in (3, 2, 1):
@@ -468,27 +522,13 @@
 
             pass_on(t, g, 0)
 
-    def final(t):
-        return remote(fin.at[t], fo.at[t], fin_s.at[t], fin_r.at[t], sibling)
+        @pl.when(jnp.logical_and(n == 8, own))
+        def _():
+            finish_own(0)
 
     @pl.when(own)
     def _():
-        for t in range(2):
-
-            @pl.loop(0, PARTS)
-            def _(n):
-                send_down(t, zl, n).wait_recv()
-                send_up(t, zl, n).wait_recv()
-
-            def summed(core):
-                some = pl.ds(pl.multiple_of(core * ch, SL), ch)
-                total = tp[t, zl, some].astype(F32) + rsd[t, zl, some].astype(F32)
-                return (total + rsu[t, zl, some].astype(F32)).astype(BF)
-
-            fin[t] = summed(1 - c)
-            final(t).start()
-            outs[t][...] = summed(c)
-
+        finish_own(1)
         for t in range(2):
             final(t).wait_send()
 
@@ -505,7 +545,7 @@
     some = pl.ds(0, ne - 1)
     ex_all = remote(rsc.at[some], rsc.at[some], ex_s, ex_r, sibling)
     ex_all.wait_recv()
-    rsc_ref[...] = rsc[...]
+    rsc_ref[...] = rsc[...].reshape(ne, 2 * ns)
     ex_all.wait_send()
     dp_all.wait_send()
     for o in results:
@@ -540,14 +580,16 @@
     def _(j):
         @pl.when(lax.rem(r - j + 8, 8) < 4)
         def _():
-            ring(j, up, up_s).wait_send()
+            for n in range(2):
+                ring(j, n, up, up_s).wait_send()
 
         @pl.when(lax.rem(j - r + 8, 8) < 3)
         def _():
-            ring(j, down, down_s).wait_send()
-
-
-def moe(nx, nq, tokens, gout, tabs, wg, wu, wd):
+            for n in range(2):
+                ring(j, n, down, down_s).wait_send()
+
+
+def moe(nx, nq, tokens, gout, ids, gates, tiles, wg, wu, wd):
     ntok = tokens.shape[0]
     ch = gout.shape[0]
     pair = 2 * ch
@@ -565,21 +607,21 @@
     return pl.pallas_call(
         functools.partial(moe_kernel, nx, nq),
         out_shape=(
-            s((ch, ntok), BF), s((ch, ntok), BF), s((2 * nq, 1, 2 * ns), F32),
+            s((ch, ntok), BF), s((ch, ntok), BF), s((2 * nq, 2 * ns), F32),
             s(wg.shape, BF), s(wu.shape, BF), s(wd.shape, BF),
         ),
-        in_specs=[hbm] * 6,
+        in_specs=[hbm, hbm, vm, vm, vm, hbm, hbm, hbm],
         out_specs=(vm, vm, vm, hbm, hbm, hbm),
         scratch_shapes=[
-            v((4, ntok, pair), BF), v((2 * nq, ntok), F32), v((4, pair, ntok), BF), wide,
+            v((4, ntok, pair), BF), v((2, 2 * nq, ntok), F32), v((2 * nq, ntok), F32), v((4, pair, ntok), BF), wide,
             v((2, 4, 2 * ns, pair), BF), v((ns, ntok), BF), v((ns, 128), F32), v((2, ns, ntok), BF),
             v(wg.shape, BF), v(wu.shape, BF), v(wd.shape, BF),
             v((2 * ns, fh), F32), v((2 * ns, fh), F32), v((2 * ns, fh), F32),
             v((2 * ns, fh), BF), v((2 * ns, fh), BF), v((2 * ns, fh), BF), v((1, 2 * ns), F32),
             wide, wide, wide, wide, tall, tall, tall, v((2, ch, ntok), BF), v((2, ch, ntok), BF),
             v((8, 1, 2 * ns), F32), v((1, 2 * ns), F32), v((2 * nq, 1, 2 * ns), F32),
-            dma((4,)), dma, dma, dma((3,)), each, each, dma((3,)),
-            dma, dma, dma, dma, dma((2, 2 * ROWBLOCKS)), dma((2, 2 * ROWBLOCKS)), dma((4,)), dma((4,)), dma((4,)),
+            dma((4,)), dma, dma((3,)), each, each, dma((3,)),
+            dma, dma, dma, dma, dma((2, 2 * ROWBLOCKS)), dma((2, 2 * ROWBLOCKS)), dma((4, 2)), dma((4, 2)), dma((4, 2)),
             each, each, each, each, each, each, each, each,
             parts, parts, parts, dma((2,)), dma((2,)), dma, dma, dma, dma,
         ],
@@ -587,42 +629,67 @@
             collective_id=1, has_side_effects=True, vmem_limit_bytes=VMEM_LIMIT
         ),
         name="moe",
-    )(tokens, gout, tabs, wg, wu, wd)
+    )(tokens, gout, ids, gates, tiles, wg, wu, wd)
+
+
+def finish_kernel(nx, nq, rsc_ref, ids_ref, gates_ref, tiles_ref, *refs):
+    count = (len(refs) - 2) // 2
+    given, gg_ref, made, sems = refs[:count], refs[count], refs[count + 1 : -1], refs[-1]
+    copies = []
+    for i in range(count):
+        step = given[i].shape[0] // 4
+        for n in range(4):
+            some = pl.ds(n * step, step)
+            copies.append(pltpu.make_async_copy(given[i].at[some], made[i].at[some], sems.at[i, n]))
+    for copy in copies:
+        copy.start()
+    me, zh, _, _ = place(nx)
+    ne = 2 * nq
+    ids = ids_ref[...]
+    names = lax.broadcasted_iota(jnp.int32, (ne, 1), 0)
+    rank, gate = routing(ids, gates_ref[...], tiles_ref[0:1, 0:1], names)
+    lane = lax.broadcasted_iota(jnp.int32, rsc_ref.shape, 1) - (zh * nq + me) * SL
+    at = jnp.zeros(rank.shape, F32)
+    for n in range(SL):
+        score = jnp.sum(jnp.where(lane == n, rsc_ref[...], 0.0), axis=1, keepdims=True)
+        at = at + jnp.where(rank == float(n), score, 0.0)
+    named = rank >= 0.0
+    at = jnp.where(named, at / jnp.where(named, gate, 1.0), 0.0)
+    for k in range(ids.shape[0]):
+        gg_ref[k : k + 1, :] = jnp.sum(jnp.where(ids[k : k + 1, :] == names, at, 0.0), axis=0, keepdims=True)
+    for copy in copies:
+        copy.wait()
+
+
+def finish(nx, nq, rsc, ids, gates, tiles, arrays):
+    hbm = pl.BlockSpec(memory_space=pl.ANY)
+    vm = pl.BlockSpec(memory_space=pltpu.VMEM)
+    s = jax.ShapeDtypeStruct
+    return pl.pallas_call(
+        functools.partial(finish_kernel, nx, nq),
+        out_shape=(s(ids.shape, F32), *(s(a.shape, a.dtype) for a in arrays)),
+        in_specs=[vm] * 4 + [hbm] * len(arrays),
+        out_specs=(vm, *([hbm] * len(arrays))),
+        scratch_shapes=[pltpu.SemaphoreType.DMA((len(arrays), 4))],
+        compiler_params=pltpu.CompilerParams(vmem_limit_bytes=16 * 1024 * 1024),
+        name="finish",
+    )(rsc, ids, gates, tiles, *arrays)
 
 
 def on_device(nx, tokens, expert_ids, gate_values, tiles, w_gate, w_up, w_down, grad_out):
-    ne = lax.axis_size("expert")
-    nq = ne // 2
-    ntok, width = tokens.shape
-    ch = grad_out.shape[1]
-    pair = 2 * ch
-    live = jnp.arange(ntok, dtype=jnp.int32) < tiles[0] * TILE
-    names = jnp.arange(ne, dtype=jnp.int32)[:, None, None]
-    chosen = (expert_ids.T[None] == names) & live[None, None, :]
-    named = jnp.any(chosen, axis=1)
-    earlier = jnp.arange(ntok)[:, None] < jnp.arange(ntok)[None, :]
-    rank = jnp.dot(named.astype(BF), earlier.astype(BF), preferred_element_type=F32)
-    rank = jnp.where(named, rank, -1.0)
-    gate = jnp.sum(jnp.where(chosen, gate_values.T[None], 0.0), axis=1)
-
-    def halves(a):
-        return a.reshape(nq // nx, 2, nx, ntok).transpose(1, 0, 2, 3).reshape(2, nq, ntok)
-
-    tabs = jnp.concatenate([halves(rank), halves(gate)], axis=1)
+    nq = lax.axis_size("expert") // 2
+    width = tokens.shape[1]
+    pair = 2 * grad_out.shape[1]
     fh = w_gate.shape[2]
+    ids = expert_ids.T
+    gates = gate_values.T
+    tiles = tiles.reshape(1, 1)
     wg = w_gate.reshape(4, pair, fh)
     wu = w_up.reshape(4, pair, fh)
-    mixed, gtok, rsc, gwg, gwu, gwd = moe(nx, nq, tokens, grad_out.T, tabs, wg, wu, w_down[0])
-    e = lax.axis_index("expert")
-    zh = (e // nx) % 2
-    me = (e // (2 * nx)) * nx + e % nx
-    mine = lax.dynamic_slice(rsc[:, 0, :], (0, zh * nq * SL + me * SL), (ne, SL))
-    slots = jnp.arange(SL, dtype=F32)
-    at = jnp.sum(jnp.where(rank[:, None, :] == slots[None, :, None], mine[:, :, None], 0.0), axis=1)
-    at = jnp.where(named, at / jnp.where(named, gate, 1.0), 0.0)
-    grad_gates = jnp.sum(jnp.where(chosen, at[:, None, :], 0.0), axis=0).T
+    mixed, gtok, rsc, *grads = moe(nx, nq, tokens, grad_out.T, ids, gates, tiles, wg, wu, w_down[0])
+    gg, mixed, gtok, gwg, gwu, gwd = finish(nx, nq, rsc, ids, gates, tiles, (mixed, gtok, *grads))
     return (
-        mixed.T, gtok.T, grad_gates,
+        mixed.T, gtok.T, gg.T,
         gwg.reshape(1, width, fh), gwu.reshape(1, width, fh), gwd[None],
     )
 

time: 170 us -> 166 us (0.976)
  local copies, waits for them, and re-layouts: 10.5 us -> 7.21 us
  other arithmetic: 3.14 us -> 0 us
  Pallas kernels: 154 us -> 157 us
    pallas_call x0 -> x1, Pallas kernels: none -> 3.4 us  [finish(): pl.pallas_call(functools.partial(finish_kernel, nx, nq), out_shape=(s(ids...]
    unnamed x11 -> x16, local copies, waits for them, and re-layouts: 9.66 us -> 7.21 us
where the time goes in v5:
time: 166 us
  Pallas kernels  157 us (95%)
  local copies, waits for them, and re-layouts  7.21 us (4%)
    pallas_call x1, Pallas kernels, moe(): pl.pallas_call(functools.partial(moe_kernel, nx, nq), out_shape=(s((ch, n...  154 us
    unnamed x16, local copies, waits for them, and re-layouts  7.21 us
    pallas_call x1, Pallas kernels, finish(): pl.pallas_call(functools.partial(finish_kernel, nx, nq), out_shape=(s(ids...  3.4 us

profile of v5, /device:TPU:97, one launch (start us, length us, event | category | flops | bytes accessed | tf_op | source)
XLA Modules:
  0.0 166.0 jit_solution(965245727494385043)
XLA Ops:
  1.3 0.0 copy-start.6
  1.3 0.0 copy-start.7
  1.3 154.0 %moe.1 = (bf16[448,256]{1,0:T(8,128)(2,1)}, bf16[448,256]{1,0:T(8,128)(2,1)}, f32[32,512]{1,0:T(8,128)}, bf16[4,896,256]{2,1,0:T(8,128)(2,1)}, bf16[4,896,256]{2,1,0:T(8,128)(2,1)}, /*index=5*/bf16[256,3584]{1,0:T(8,128)(2,1)}) custom-call(bf16[256,3584]{1,0:T(8,128)(2,1)} %tok_ref.1, bf16[448,256]{1,0:T(8,128)(2,1)} %bitcast.22, s32[8,256]{1,0:T(8,128)} %bitcast.15, ...), custom_call_target="tpu_custom_call" | custom-call | tf_op jit(solution)/shard_map/moe/pallas_call | solution.py:607
  155.3 0.0 copy-done.6
  155.3 0.0 copy-done.7
  155.3 0.0 copy-start
  155.4 1.5 copy-done
  156.8 0.0 copy-start.1
  156.9 1.5 copy-done.1
  158.3 0.0 copy-start.2
  158.4 1.5 copy-done.2
  159.8 0.0 copy-start.3
  159.9 0.9 copy-done.3
  160.8 0.0 copy-start.4
  160.8 0.9 copy-done.4
  161.7 0.0 copy-start.5
  161.7 0.8 copy-done.5
  162.6 3.4 %finish.1 = (f32[8,256]{1,0:T(8,128)}, bf16[448,256]{1,0:T(8,128)(2,1)}, bf16[448,256]{1,0:T(8,128)(2,1)}, bf16[4,896,256]{2,1,0:T(8,128)(2,1)}, bf16[4,896,256]...) custom-call(f32[32,512]{1,0:T(8,128)S(1)} %copy-done.5, s32[8,256]{1,0:T(8,128)S(1)} %bitcast.16, f32[8,256]{1,0:T(8,128)S(1)} %bitcast.18, ...), custom_call_target="tpu_custom_call" | custom-call | tf_op jit(solution)/shard_map/finish/pallas_call | solution.py:668
Async XLA Ops:
  1.3 154.1 %copy-start.6 = (s32[256,8]{0,1:T(8,128)S(1)}, s32[256,8]{0,1:T(8,128)}, u32[]{:S(2)}) copy-start(s32[256,8]{0,1:T(8,128)} %param.9) | copy-start | bytes 24580
  1.3 154.1 %copy-start.7 = (f32[256,8]{0,1:T(8,128)S(1)}, f32[256,8]{0,1:T(8,128)}, u32[]{:S(2)}) copy-start(f32[256,8]{0,1:T(8,128)} %param.10) | copy-start | bytes 24580
  155.3 1.5 copy-start
  156.8 1.5 copy-start.1
  158.3 1.5 copy-start.2
  159.8 0.9 copy-start.3
  160.8 0.9 copy-start.4
  161.7 0.8 copy-start.5

commit v6 on v5

--- a/solution.py
+++ b/solution.py
@@ -380,6 +380,73 @@
 
     send_back(0)
 
+    def rows_of(n):
+        return pl.ds(pl.multiple_of(n * part, SL), part)
+
+    def send_down(t, j, n):
+        return remote(
+            tp.at[t, j, rows_of(n)], rsd.at[t, j, rows_of(n)], ring_s.at[t, j, n], down_r.at[t, j, n], down
+        )
+
+    def send_up(t, j, n):
+        return remote(
+            tp.at[t, j, rows_of(n)], rsu.at[t, j, rows_of(n)], ring_s.at[t, j, n], up_r.at[t, j, n], up
+        )
+
+    def add_in(t, j, n, a):
+        tp[t, j, rows_of(n)] = (
+            tp[t, j, rows_of(n)].astype(F32) + a[t, j, rows_of(n)].astype(F32)
+        ).astype(BF)
+
+    def pass_on(t, g, m):
+        above = lax.rem(r - g + 8, 8)
+        below = lax.rem(g - r + 8, 8)
+
+        @pl.when(above == 4 - m)
+        def _():
+            @pl.loop(0, PARTS)
+            def _(n):
+                if m > 0:
+                    send_down(t, g, n).wait_recv()
+                    add_in(t, g, n, rsd)
+                send_down(t, g, n).start()
+
+        if m < 3:
+
+            @pl.when(below == 3 - m)
+            def _():
+                @pl.loop(0, PARTS)
+                def _(n):
+                    if m > 0:
+                        send_up(t, g, n).wait_recv()
+                        add_in(t, g, n, rsu)
+                    send_up(t, g, n).start()
+
+    def return_step(n):
+        for m in (3, 2, 1):
+            at = n - m
+
+            @pl.when(jnp.logical_and(at >= 0, at < 8))
+            def _():
+                pass_on(lax.div(at, 4), lax.rem(at, 4), m)
+
+        @pl.when(n < 8)
+        def _():
+            t = lax.div(n, 4)
+            g = lax.rem(n, 4)
+            back_arrived(t, g).wait_recv()
+            back_local(t, g).wait()
+
+            @pl.when(t == 0)
+            def _():
+                tp[0, g] = (tdot(rv[0, g], wt[0]) + tdot(rv[0, g], wt[1])).astype(BF)
+
+            @pl.when(t == 1)
+            def _():
+                tp[1, g] = tdot(rv[1, g], pick[...]).astype(BF)
+
+            pass_on(t, g, 0)
+
     take_in(1)
     dacc[...] = jnp.zeros_like(dacc)
     for f in range(4):
@@ -408,6 +475,7 @@
         so[1, f] = (dot_t(dgb[theirs, :], wg[f]) + dot_t(dub[theirs, :], wu[f])).astype(BF)
         to_sibling(1, f).start()
         ob[1, f] = (dot_t(dgb[mine, :], wg[f]) + dot_t(dub[mine, :], wu[f])).astype(BF)
+        return_step(f)
 
     send_back(1)
 
@@ -421,63 +489,6 @@
     def _(i):
         remote(st, rsc.at[e], ex_s, ex_r, {"expert": lax.rem(e + i, ne), "dp": d}).start()
 
-    @pl.loop(0, 4)
-    def _(f):
-        wg[f] = tdot(xdy[0, f], dgb[...]).astype(BF)
-        wu[f] = tdot(xdy[0, f], dub[...]).astype(BF)
-
-    for f in range(4):
-        wd[:, lanes(f)] = tdot(hb[...], xdy[1, f]).astype(BF)
-
-    results = [
-        pltpu.make_async_copy(a, b, out_l.at[i])
-        for i, (a, b) in enumerate(((wg, gwg_ref), (wu, gwu_ref), (wd, gwd_ref)))
-    ]
-    for o in results:
-        o.start()
-
-    def rows_of(n):
-        return pl.ds(pl.multiple_of(n * part, SL), part)
-
-    def send_down(t, j, n):
-        return remote(
-            tp.at[t, j, rows_of(n)], rsd.at[t, j, rows_of(n)], ring_s.at[t, j, n], down_r.at[t, j, n], down
-        )
-
-    def send_up(t, j, n):
-        return remote(
-            tp.at[t, j, rows_of(n)], rsu.at[t, j, rows_of(n)], ring_s.at[t, j, n], up_r.at[t, j, n], up
-        )
-
-    def add_in(t, j, n, a):
-        tp[t, j, rows_of(n)] = (
-            tp[t, j, rows_of(n)].astype(F32) + a[t, j, rows_of(n)].astype(F32)
-        ).astype(BF)
-
-    def pass_on(t, g, m):
-        above = lax.rem(r - g + 8, 8)
-        below = lax.rem(g - r + 8, 8)
-
-        @pl.when(above == 4 - m)
-        def _():
-            @pl.loop(0, PARTS)
-            def _(n):
-                if m > 0:
-                    send_down(t, g, n).wait_recv()
-                    add_in(t, g, n, rsd)
-                send_down(t, g, n).start()
-
-        if m < 3:
-
-            @pl.when(below == 3 - m)
-            def _():
-                @pl.loop(0, PARTS)
-                def _(n):
-                    if m > 0:
-                        send_up(t, g, n).wait_recv()
-                        add_in(t, g, n, rsu)
-                    send_up(t, g, n).start()
-
     def final(t):
         return remote(fin.at[t], fo.at[t], fin_s.at[t], fin_r.at[t], sibling)
 
@@ -496,35 +507,31 @@
         final(t).start()
         outs[t][...] = summed(c)
 
-    @pl.loop(0, 11)
+    results = [
+        pltpu.make_async_copy(a, b, out_l.at[i])
+        for i, (a, b) in enumerate(((wg, gwg_ref), (wu, gwu_ref), (wd, gwd_ref)))
+    ]
+
+    @pl.loop(4, 11)
     def _(n):
-        for m in (3, 2, 1):
-            at = n - m
-
-            @pl.when(jnp.logical_and(at >= 0, at < 8))
-            def _():
-                pass_on(lax.div(at, 4), lax.rem(at, 4), m)
+        return_step(n)
 
         @pl.when(n < 8)
         def _():
-            t = lax.div(n, 4)
-            g = lax.rem(n, 4)
-            back_arrived(t, g).wait_recv()
-            back_local(t, g).wait()
-
-            @pl.when(t == 0)
-            def _():
-                tp[0, g] = (tdot(rv[0, g], wt[0]) + tdot(rv[0, g], wt[1])).astype(BF)
-
-            @pl.when(t == 1)
-            def _():
-                tp[1, g] = tdot(rv[1, g], pick[...]).astype(BF)
-
-            pass_on(t, g, 0)
-
-        @pl.when(jnp.logical_and(n == 8, own))
-        def _():
-            finish_own(0)
+            f = n - 4
+            some = pl.ds(pl.multiple_of(f * pair, 128), pair)
+            wg[f] = tdot(xdy[0, f], dgb[...]).astype(BF)
+            wu[f] = tdot(xdy[0, f], dub[...]).astype(BF)
+            wd[:, some] = tdot(hb[...], xdy[1, f]).astype(BF)
+
+        @pl.when(n == 8)
+        def _():
+            for o in results:
+                o.start()
+
+            @pl.when(own)
+            def _():
+                finish_own(0)
 
     @pl.when(own)
     def _():
@@ -671,7 +678,7 @@
         in_specs=[vm] * 4 + [hbm] * len(arrays),
         out_specs=(vm, *([hbm] * len(arrays))),
         scratch_shapes=[pltpu.SemaphoreType.DMA((len(arrays), 4))],
-        compiler_params=pltpu.CompilerParams(vmem_limit_bytes=16 * 1024 * 1024),
+        compiler_params=pltpu.CompilerParams(vmem_limit_bytes=VMEM_LIMIT),
         name="finish",
     )(rsc, ids, gates, tiles, *arrays)
 

time: 166 us -> 333 us (2.01)
  Pallas kernels: 157 us -> 331 us
  local copies, waits for them, and re-layouts: 7.21 us -> 0 us
    pallas_call x1, Pallas kernels: 3.4 us -> 183 us  [finish(): pl.pallas_call(functools.partial(finish_kernel, nx, nq), out_shape=(s(ids...]
    unnamed x16 -> x0, local copies, waits for them, and re-layouts: 7.21 us -> none
    pallas_call x1, Pallas kernels: 154 us -> 148 us  [moe(): pl.pallas_call(functools.partial(moe_kernel, nx, nq), out_shape=(s((ch, n...]
where the time goes in v6:
time: 333 us
  Pallas kernels  331 us (99%)
    pallas_call x1, Pallas kernels, finish(): pl.pallas_call(functools.partial(finish_kernel, nx, nq), out_shape=(s(ids...  183 us
    pallas_call x1, Pallas kernels, moe(): pl.pallas_call(functools.partial(moe_kernel, nx, nq), out_shape=(s((ch, n...  148 us

profile of v6, /device:TPU:97, one launch (start us, length us, event | category | flops | bytes accessed | tf_op | source)
XLA Modules:
  0.0 332.6 jit_solution(15654228097647279863)
XLA Ops:
  1.3 147.9 %moe.1 = (bf16[448,256]{1,0:T(8,128)(2,1)}, bf16[448,256]{1,0:T(8,128)(2,1)}, f32[32,512]{1,0:T(8,128)}, bf16[4,896,256]{2,1,0:T(8,128)(2,1)}, bf16[4,896,256]{2,1,0:T(8,128)(2,1)}, /*index=5*/bf16[256,3584]{1,0:T(8,128)(2,1)}) custom-call(bf16[256,3584]{1,0:T(8,128)(2,1)} %tok_ref.1, bf16[448,256]{1,0:T(8,128)(2,1)} %bitcast.18, s32[8,256]{1,0:T(8,128)} %bitcast.19, ...), custom_call_target="tpu_custom_call" | custom-call | tf_op jit(solution)/shard_map/moe/pallas_call | solution.py:614
  149.2 183.4 %finish.1 = (f32[8,256]{1,0:T(8,128)}, bf16[448,256]{1,0:T(8,128)(2,1)}, bf16[448,256]{1,0:T(8,128)(2,1)}, bf16[4,896,256]{2,1,0:T(8,128)(2,1)}, bf16[4,896,256]...) custom-call(f32[32,512]{1,0:T(8,128)} %get-tuple-element.18.rsc_ref, s32[8,256]{1,0:T(8,128)} %bitcast.20, f32[8,256]{1,0:T(8,128)} %bitcast.22, ...), custom_call_target="tpu_custom_call" | custom-call | tf_op jit(solution)/shard_map/finish/pallas_call | solution.py:675

commit v7 on v6

--- a/solution.py
+++ b/solution.py
@@ -339,21 +339,19 @@
         some = pl.ds(0, ns - SL)
         return remote(ob.at[t, g, some], rv.at[t, g, some], back_s.at[t, g], back_r.at[t, g], sibling)
 
-    def send_back(t):
-        @pl.loop(0, 4)
-        def _(g):
-            to_sibling(t, g).wait_recv()
-            ob[t, g] = (ob[t, g].astype(F32) + rb[t, g].astype(F32)).astype(BF)
-
-            @pl.loop(1, nq)
-            def _(i):
-                q = lax.rem(me + i, nq)
-                remote(
-                    ob.at[t, g, slots(q)], rv.at[t, g, slots(me)],
-                    back_s.at[t, g], back_r.at[t, g], device(nx, q, z, c),
-                ).start()
-
-            back_local(t, g).start()
+    def send_back(t, g):
+        to_sibling(t, g).wait_recv()
+        ob[t, g] = (ob[t, g].astype(F32) + rb[t, g].astype(F32)).astype(BF)
+
+        @pl.loop(1, nq)
+        def _(i):
+            q = lax.rem(me + i, nq)
+            remote(
+                ob.at[t, g, slots(q)], rv.at[t, g, slots(me)],
+                back_s.at[t, g], back_r.at[t, g], device(nx, q, z, c),
+            ).start()
+
+        back_local(t, g).start()
 
     def lanes(f):
         return slice(f * pair, (f + 1) * pair)
@@ -378,7 +376,9 @@
         to_sibling(0, f).start()
         ob[0, f] = jnp.dot(hb[mine, :], wd[:, lanes(f)], preferred_element_type=F32).astype(BF)
 
-    send_back(0)
+    @pl.loop(0, 4)
+    def _(f):
+        send_back(0, f)
 
     def rows_of(n):
         return pl.ds(pl.multiple_of(n * part, SL), part)
@@ -475,9 +475,14 @@
         so[1, f] = (dot_t(dgb[theirs, :], wg[f]) + dot_t(dub[theirs, :], wu[f])).astype(BF)
         to_sibling(1, f).start()
         ob[1, f] = (dot_t(dgb[mine, :], wg[f]) + dot_t(dub[mine, :], wu[f])).astype(BF)
+
+        @pl.when(f > 0)
+        def _():
+            send_back(1, f - 1)
+
         return_step(f)
 
-    send_back(1)
+    send_back(1, 3)
 
     seven = scr.at[pl.ds(0, 7)]
     dp_all = remote(seven, seven, dp_s, dp_r, sibling)
@@ -640,16 +645,21 @@
 
 
 def finish_kernel(nx, nq, rsc_ref, ids_ref, gates_ref, tiles_ref, *refs):
-    count = (len(refs) - 2) // 2
-    given, gg_ref, made, sems = refs[:count], refs[count], refs[count + 1 : -1], refs[-1]
-    copies = []
+    count = (len(refs) - 3) // 3
+    given, gg_ref, made = refs[:count], refs[count], refs[count + 1 : 2 * count + 1]
+    held, got, put = refs[2 * count + 1 : -2], refs[-2], refs[-1]
+    loads, stores = [], []
     for i in range(count):
         step = given[i].shape[0] // 4
         for n in range(4):
             some = pl.ds(n * step, step)
-            copies.append(pltpu.make_async_copy(given[i].at[some], made[i].at[some], sems.at[i, n]))
-    for copy in copies:
+            loads.append(pltpu.make_async_copy(given[i].at[some], held[i].at[some], got.at[i, n]))
+            stores.append(pltpu.make_async_copy(held[i].at[some], made[i].at[some], put.at[i, n]))
+    for copy in loads:
         copy.start()
+    for load, store in zip(loads, stores):
+        load.wait()
+        store.start()
     me, zh, _, _ = place(nx)
     ne = 2 * nq
     ids = ids_ref[...]
@@ -664,8 +674,8 @@
     at = jnp.where(named, at / jnp.where(named, gate, 1.0), 0.0)
     for k in range(ids.shape[0]):
         gg_ref[k : k + 1, :] = jnp.sum(jnp.where(ids[k : k + 1, :] == names, at, 0.0), axis=0, keepdims=True)
-    for copy in copies:
-        copy.wait()
+    for store in stores:
+        store.wait()
 
 
 def finish(nx, nq, rsc, ids, gates, tiles, arrays):
@@ -677,7 +687,10 @@
         out_shape=(s(ids.shape, F32), *(s(a.shape, a.dtype) for a in arrays)),
         in_specs=[vm] * 4 + [hbm] * len(arrays),
         out_specs=(vm, *([hbm] * len(arrays))),
-        scratch_shapes=[pltpu.SemaphoreType.DMA((len(arrays), 4))],
+        scratch_shapes=[
+            *(pltpu.VMEM(a.shape, a.dtype) for a in arrays),
+            pltpu.SemaphoreType.DMA((len(arrays), 4)), pltpu.SemaphoreType.DMA((len(arrays), 4)),
+        ],
         compiler_params=pltpu.CompilerParams(vmem_limit_bytes=VMEM_LIMIT),
         name="finish",
     )(rsc, ids, gates, tiles, *arrays)

time: 333 us -> 155 us (0.47)
  Pallas kernels: 331 us -> 152 us
    pallas_call x1, Pallas kernels: 183 us -> 6.86 us  [finish(): pl.pallas_call(functools.partial(finish_kernel, nx, nq), out_shape=(s(ids...]
where the time goes in v7:
time: 155 us; the launch traced here: 154 us
  Pallas kernels  152 us (98%)
    pallas_call x1, Pallas kernels, moe(): pl.pallas_call(functools.partial(moe_kernel, nx, nq), out_shape=(s((ch, n...  145 us
    pallas_call x1, Pallas kernels, finish(): pl.pallas_call(functools.partial(finish_kernel, nx, nq), out_shape=(s(ids...  6.86 us

profile of v7, /device:TPU:97, one launch (start us, length us, event | category | flops | bytes accessed | tf_op | source)
XLA Modules:
  0.0 153.6 jit_solution(13754913598998658665)
XLA Ops:
  1.3 145.5 %moe.1 = (bf16[448,256]{1,0:T(8,128)(2,1)}, bf16[448,256]{1,0:T(8,128)(2,1)}, f32[32,512]{1,0:T(8,128)}, bf16[4,896,256]{2,1,0:T(8,128)(2,1)}, bf16[4,896,256]{2,1,0:T(8,128)(2,1)}, /*index=5*/bf16[256,3584]{1,0:T(8,128)(2,1)}) custom-call(bf16[256,3584]{1,0:T(8,128)(2,1)} %tok_ref.1, bf16[448,256]{1,0:T(8,128)(2,1)} %bitcast.18, s32[8,256]{1,0:T(8,128)} %bitcast.19, ...), custom_call_target="tpu_custom_call" | custom-call | tf_op jit(solution)/shard_map/moe/pallas_call | solution.py:619
  146.8 6.9 %finish.1 = (f32[8,256]{1,0:T(8,128)}, bf16[448,256]{1,0:T(8,128)(2,1)}, bf16[448,256]{1,0:T(8,128)(2,1)}, bf16[4,896,256]{2,1,0:T(8,128)(2,1)}, bf16[4,896,256]...) custom-call(f32[32,512]{1,0:T(8,128)} %get-tuple-element.18.rsc_ref, s32[8,256]{1,0:T(8,128)} %bitcast.20, f32[8,256]{1,0:T(8,128)} %bitcast.22, ...), custom_call_target="tpu_custom_call" | custom-call | tf_op jit(solution)/shard_map/finish/pallas_call | solution.py:685

commit v8 on v7

--- a/solution.py
+++ b/solution.py
@@ -16,7 +16,8 @@
 ROWBLOCKS = 4
 PARTS = 4
 SKEW = 3
-RING_FIRST = 6
+RING_FIRST = 9
+RING_GAP = 2
 
 
 def place(nx):
@@ -286,6 +287,8 @@
 
     @pl.when(other)
     def _():
+        inside = min(7, -(-(pieces + 4 * SKEW - RING_FIRST) // RING_GAP))
+
         @pl.loop(SKEW, pieces + 4 * SKEW)
         def _(n):
             for h, far, who in ((0, r - 3, up), (1, 8 - r, down)):
@@ -308,12 +311,15 @@
                     x_group(2 * h + lax.div(i, ROWBLOCKS))
 
             at = n - RING_FIRST
-
-            @pl.when(jnp.logical_and(at >= 0, lax.rem(at + 8, 2) == 0))
-            def _():
-                ring_step(lax.div(at, 4) + 1, lax.div(lax.rem(at, 4), 2))
-
-        ring_step(4, 1)
+            turn = lax.div(at, RING_GAP)
+
+            @pl.when(jnp.logical_and(at >= 0, jnp.logical_and(turn < inside, lax.rem(at + 8 * RING_GAP, RING_GAP) == 0)))
+            def _():
+                ring_step(lax.div(turn, 2) + 1, lax.rem(turn, 2))
+
+        @pl.loop(inside, 8)
+        def _(turn):
+            ring_step(lax.div(turn, 2) + 1, lax.rem(turn, 2))
 
     def share(t, g):
         return remote(xdy.at[t, g, mine], xdy.at[t, g, mine], share_s.at[t, g], share_r.at[t, g], sibling)
@@ -657,9 +663,6 @@
             stores.append(pltpu.make_async_copy(held[i].at[some], made[i].at[some], put.at[i, n]))
     for copy in loads:
         copy.start()
-    for load, store in zip(loads, stores):
-        load.wait()
-        store.start()
     me, zh, _, _ = place(nx)
     ne = 2 * nq
     ids = ids_ref[...]
@@ -674,6 +677,9 @@
     at = jnp.where(named, at / jnp.where(named, gate, 1.0), 0.0)
     for k in range(ids.shape[0]):
         gg_ref[k : k + 1, :] = jnp.sum(jnp.where(ids[k : k + 1, :] == names, at, 0.0), axis=0, keepdims=True)
+    for load, store in zip(loads, stores):
+        load.wait()
+        store.start()
     for store in stores:
         store.wait()
 

time: 155 us -> 150 us (0.968)
  Pallas kernels: 152 us -> 148 us
    pallas_call x1, Pallas kernels: 145 us -> 141 us  [moe(): pl.pallas_call(functools.partial(moe_kernel, nx, nq), out_shape=(s((ch, n...]
where the time goes in v8:
time: 150 us; the launch traced here: 149 us
  Pallas kernels  148 us (99%)
    pallas_call x1, Pallas kernels, moe(): pl.pallas_call(functools.partial(moe_kernel, nx, nq), out_shape=(s((ch, n...  141 us
    pallas_call x1, Pallas kernels, finish(): pl.pallas_call(functools.partial(finish_kernel, nx, nq), out_shape=(s(ids...  6.87 us

profile of v8, /device:TPU:97, one launch (start us, length us, event | category | flops | bytes accessed | tf_op | source)
XLA Modules:
  0.0 148.9 jit_solution(3910718870794619725)
XLA Ops:
  1.3 140.7 %moe.1 = (bf16[448,256]{1,0:T(8,128)(2,1)}, bf16[448,256]{1,0:T(8,128)(2,1)}, f32[32,512]{1,0:T(8,128)}, bf16[4,896,256]{2,1,0:T(8,128)(2,1)}, bf16[4,896,256]{2,1,0:T(8,128)(2,1)}, /*index=5*/bf16[256,3584]{1,0:T(8,128)(2,1)}) custom-call(bf16[256,3584]{1,0:T(8,128)(2,1)} %tok_ref.1, bf16[448,256]{1,0:T(8,128)(2,1)} %bitcast.18, s32[8,256]{1,0:T(8,128)} %bitcast.19, ...), custom_call_target="tpu_custom_call" | custom-call | tf_op jit(solution)/shard_map/moe/pallas_call | solution.py:625
  142.0 6.9 %finish.1 = (f32[8,256]{1,0:T(8,128)}, bf16[448,256]{1,0:T(8,128)(2,1)}, bf16[448,256]{1,0:T(8,128)(2,1)}, bf16[4,896,256]{2,1,0:T(8,128)(2,1)}, bf16[4,896,256]...) custom-call(f32[32,512]{1,0:T(8,128)} %get-tuple-element.18.rsc_ref, s32[8,256]{1,0:T(8,128)} %bitcast.20, f32[8,256]{1,0:T(8,128)} %bitcast.22, ...), custom_call_target="tpu_custom_call" | custom-call | tf_op jit(solution)/shard_map/finish/pallas_call | solution.py:691

commit v9 on v8

--- a/solution.py
+++ b/solution.py
@@ -14,7 +14,7 @@
 BF = jnp.bfloat16
 F32 = jnp.float32
 ROWBLOCKS = 4
-PARTS = 4
+PARTS = 8
 SKEW = 3
 RING_FIRST = 9
 RING_GAP = 2

time: 150 us -> 150 us (level)
  no operation moved by 1% of the time
where the time goes in v9:
time: 150 us
  Pallas kernels  148 us (99%)
    pallas_call x1, Pallas kernels, moe(): pl.pallas_call(functools.partial(moe_kernel, nx, nq), out_shape=(s((ch, n...  142 us
    pallas_call x1, Pallas kernels, finish(): pl.pallas_call(functools.partial(finish_kernel, nx, nq), out_shape=(s(ids...  6.87 us

profile of v9, /device:TPU:97, one launch (start us, length us, event | category | flops | bytes accessed | tf_op | source)
XLA Modules:
  0.0 149.7 jit_solution(17011965903390518213)
XLA Ops:
  1.3 141.6 %moe.1 = (bf16[448,256]{1,0:T(8,128)(2,1)}, bf16[448,256]{1,0:T(8,128)(2,1)}, f32[32,512]{1,0:T(8,128)}, bf16[4,896,256]{2,1,0:T(8,128)(2,1)}, bf16[4,896,256]{2,1,0:T(8,128)(2,1)}, /*index=5*/bf16[256,3584]{1,0:T(8,128)(2,1)}) custom-call(bf16[256,3584]{1,0:T(8,128)(2,1)} %tok_ref.1, bf16[448,256]{1,0:T(8,128)(2,1)} %bitcast.18, s32[8,256]{1,0:T(8,128)} %bitcast.19, ...), custom_call_target="tpu_custom_call" | custom-call | tf_op jit(solution)/shard_map/moe/pallas_call | solution.py:625
  142.8 6.9 %finish.1 = (f32[8,256]{1,0:T(8,128)}, bf16[448,256]{1,0:T(8,128)(2,1)}, bf16[448,256]{1,0:T(8,128)(2,1)}, bf16[4,896,256]{2,1,0:T(8,128)(2,1)}, bf16[4,896,256]...) custom-call(f32[32,512]{1,0:T(8,128)} %get-tuple-element.18.rsc_ref, s32[8,256]{1,0:T(8,128)} %bitcast.20, f32[8,256]{1,0:T(8,128)} %bitcast.22, ...), custom_call_target="tpu_custom_call" | custom-call | tf_op jit(solution)/shard_map/finish/pallas_call | solution.py:691
